TPU v7x, 128 devices: a whole 4x4x4 slice. The times are simulated.
128 devices in a mesh: fr: 4 (over x_hi, core), fc: 32 (over z, x_lo, y).
Axes of the slice: x: 4 (x_hi: 2, x_lo: 2; x = x_hi * 2 + x_lo), y: 4, z: 4, core: 2. Of those that a mesh axis runs over, the one named last changes fastest.
Arguments:
- front_slab: float32 [2048, 98304], P('fr', 'fc'), may hold values from -6 to 6
- panels: float32 [4, 98304, 256], P(None, 'fc'), may hold values from -8 to 8
- diagonal_blocks: float32 [4, 256, 256], P(None, None, 'fc'), may hold values from -3 to 96, as said below
- extend_maps: int32 [4, 4, 32, 128], P(None, 'fr', 'fc'), may hold values from 0 to 127, each once within a row
Outputs:
- front_out: float32 [2048, 98304], P('fr', 'fc')
Inputs may be any that keep to these rules, and one draw needn't show every extreme that they name: `extend_maps`: each level's map at each grid position names every row of the block once. `diagonal_blocks`: the symmetric part of each block is positive definite.
All inputs are finite; a program needn't handle non-finite values.
Results may differ from a plain program's by a relative error of at most 0.0001.
Values sent between devices are 32-bit elements; how exact they have to be, the bound alone decides.
No kernel may reach another device: no remote copies, remote signals or barrier semaphores. Data moves between devices by JAX's collectives and lax.ppermute only.
A program may use at most 128 MiB of HBM per device.

v0:
```python
import jax
import jax.numpy as jnp
from jax import lax
from jax.sharding import PartitionSpec as P

HIGHEST = lax.Precision.HIGHEST


def partner(x, axis, distance):
    return lax.ppermute(x, axis, [(i, i ^ 1 << distance) for i in range(lax.axis_size(axis))])


def broadcast(block, axis, source):
    block = jnp.where(lax.axis_index(axis) == source, block, jnp.zeros_like(block))
    return lax.psum(block, axis)


def inverse_factor(diagonal_block):
    symmetric = 0.5 * (diagonal_block + diagonal_block.T)
    lower_factor = jnp.linalg.cholesky(symmetric)
    identity = jnp.eye(symmetric.shape[0], dtype=symmetric.dtype)
    return lax.linalg.triangular_solve(lower_factor, identity, left_side=True, lower=True)


def swap_columns(top_rows, bit_index):
    return partner(top_rows, "fc", bit_index)


def swap_rows(top_rows, bit_index):
    return partner(top_rows, "fr", bit_index)


def merge_top(front_slab, received, row_map):
    block_rows = row_map.shape[0]
    moved_rows = jnp.take(received, row_map, axis=0)
    return lax.dynamic_update_slice(front_slab, front_slab[:block_rows] + moved_rows, (0, 0))


def body(front_slab, panels, diagonal_blocks, extend_maps):
    row_count, col_count = front_slab.shape
    block_rows = extend_maps.shape[3]
    row_index = lax.axis_index("fr")
    row_devices = lax.axis_size("fr")
    col_devices = lax.axis_size("fc")
    whole_diagonal = lax.all_gather(diagonal_blocks, "fc", axis=2, tiled=True)
    partner_plan = [
        (True, col_devices.bit_length() - 2),
        (True, 0),
        (False, row_devices.bit_length() - 2),
        (False, 0),
    ]
    pending = None
    for level_index in range(4):
        use_columns, bit_index = partner_plan[level_index]
        top_rows = front_slab[:block_rows]
        received = (
            swap_columns(top_rows, bit_index) if use_columns else swap_rows(top_rows, bit_index)
        )
        front_slab = merge_top(front_slab, received, extend_maps[level_index, 0, 0])
        inverse = inverse_factor(whole_diagonal[level_index])
        panel_level = panels[level_index]
        column_factor = jnp.dot(panel_level, inverse.T, precision=HIGHEST)
        first_row = row_index * row_count
        source = lax.dynamic_slice_in_dim(column_factor, first_row % col_count, row_count, 0)
        slab_factor = broadcast(source, "fc", first_row // col_count)
        front_slab = front_slab - jnp.dot(slab_factor, column_factor.T, precision=HIGHEST)
    return front_slab


def solution(mesh):
    in_specs = (P("fr", "fc"), P(None, "fc", None), P(None, None, "fc"), P(None, "fr", "fc", None))
    out_specs = P("fr", "fc")
    return jax.shard_map(body, mesh=mesh, in_specs=in_specs, out_specs=out_specs, check_vma=False)
```

profile of v0, /device:TPU:1, one launch (start us, length us, event | category | flops | bytes accessed | tf_op | source)
XLA Modules:
  0.0 866.0 jit_solution(11738925772173782008)
XLA Ops:
  20.7 126.8 %all-gather.2.cloned.1.call-done = f32[4,256,256]{1,0,2:T(4,128)} async-done(((f32[4,256,8]{1,0,2:T(4,128)}), f32[4,256,256]{1,0,2:T(4,128)}) %all-gather.2.cloned.1.call-update) | async-done | bytes 1048592 | tf_op jit(solution)/shard_map/all_gather | solution.py:45
  154.1 11.7 %cholesky.214 = f32[128,128]{1,0:T(8,128)S(1)} custom-call(f32[128,128]{1,0:T(8,128)S(1)} %cholesky.346), custom_call_target="Cholesky" | custom-call | tf_op jit(solution)/shard_map/jit(cholesky)/cholesky | solution.py:20
  165.8 9.8 %custom-call.17 = f32[1,128,128]{1,2,0:T(8,128)S(1)} custom-call(f32[1,128,128]{2,1,0:T(8,128)S(1)} %get-tuple-element.109), custom_call_target="InvertDiagBlocksLowerTriangular" | custom-call | tf_op jit(solution)/shard_map/jit(cholesky)/cholesky | solution.py:20
  176.1 11.7 %cholesky.231 = f32[128,128]{1,0:T(8,128)S(1)} custom-call(f32[128,128]{1,0:T(8,128)S(1)} %convolution_subtract_fusion.11), custom_call_target="Cholesky" | custom-call | tf_op jit(solution)/shard_map/jit(cholesky)/cholesky | solution.py:20
  194.6 20.0 %custom-call.18 = f32[2,128,128]{1,2,0:T(8,128)S(1)} custom-call(f32[2,128,128]{2,1,0:T(8,128)S(1)} %get-tuple-element.34), custom_call_target="InvertDiagBlocksLowerTriangular" | custom-call | tf_op jit(solution)/shard_map/triangular_solve/custom-call.0 | solution.py:22
  215.7 11.7 %cholesky.248 = f32[128,128]{1,0:T(8,128)S(1)} custom-call(f32[128,128]{1,0:T(8,128)S(1)} %cholesky.349), custom_call_target="Cholesky" | custom-call | tf_op jit(solution)/shard_map/jit(cholesky)/cholesky | solution.py:20
  227.5 9.8 %custom-call.19 = f32[1,128,128]{1,2,0:T(8,128)S(1)} custom-call(f32[1,128,128]{2,1,0:T(8,128)S(1)} %get-tuple-element.105), custom_call_target="InvertDiagBlocksLowerTriangular" | custom-call | tf_op jit(solution)/shard_map/jit(cholesky)/cholesky | solution.py:20
  237.8 11.7 %cholesky.265 = f32[128,128]{1,0:T(8,128)S(1)} custom-call(f32[128,128]{1,0:T(8,128)S(1)} %convolution_subtract_fusion.10), custom_call_target="Cholesky" | custom-call | tf_op jit(solution)/shard_map/jit(cholesky)/cholesky | solution.py:20
  256.5 19.8 %custom-call.20 = f32[2,128,128]{1,2,0:T(8,128)S(1)} custom-call(f32[2,128,128]{2,1,0:T(8,128)S(1)} %get-tuple-element.35), custom_call_target="InvertDiagBlocksLowerTriangular" | custom-call | tf_op jit(solution)/shard_map/triangular_solve/custom-call.0 | solution.py:22
  290.5 11.7 %cholesky.282 = f32[128,128]{1,0:T(8,128)S(1)} custom-call(f32[128,128]{1,0:T(8,128)S(1)} %cholesky.352), custom_call_target="Cholesky" | custom-call | tf_op jit(solution)/shard_map/jit(cholesky)/cholesky | solution.py:20
  302.3 10.0 %custom-call.21 = f32[1,128,128]{1,2,0:T(8,128)S(1)} custom-call(f32[1,128,128]{2,1,0:T(8,128)S(1)} %get-tuple-element.101), custom_call_target="InvertDiagBlocksLowerTriangular" | custom-call | tf_op jit(solution)/shard_map/jit(cholesky)/cholesky | solution.py:20
  312.8 11.7 %cholesky.299 = f32[128,128]{1,0:T(8,128)S(1)} custom-call(f32[128,128]{1,0:T(8,128)S(1)} %convolution_subtract_fusion.9), custom_call_target="Cholesky" | custom-call | tf_op jit(solution)/shard_map/jit(cholesky)/cholesky | solution.py:20
  331.5 20.1 %custom-call.22 = f32[2,128,128]{1,2,0:T(8,128)S(1)} custom-call(f32[2,128,128]{2,1,0:T(8,128)S(1)} %get-tuple-element.36), custom_call_target="InvertDiagBlocksLowerTriangular" | custom-call | tf_op jit(solution)/shard_map/triangular_solve/custom-call.0 | solution.py:22
  359.0 11.7 %cholesky.316 = f32[128,128]{1,0:T(8,128)S(1)} custom-call(f32[128,128]{1,0:T(8,128)S(1)} %cholesky.355), custom_call_target="Cholesky" | custom-call | tf_op jit(solution)/shard_map/jit(cholesky)/cholesky | solution.py:20
  370.8 9.8 %custom-call.23 = f32[1,128,128]{1,2,0:T(8,128)S(1)} custom-call(f32[1,128,128]{2,1,0:T(8,128)S(1)} %get-tuple-element.97), custom_call_target="InvertDiagBlocksLowerTriangular" | custom-call | tf_op jit(solution)/shard_map/jit(cholesky)/cholesky | solution.py:20
  381.1 11.9 %cholesky.333 = f32[128,128]{1,0:T(8,128)S(1)} custom-call(f32[128,128]{1,0:T(8,128)S(1)} %convolution_subtract_fusion.8), custom_call_target="Cholesky" | custom-call | tf_op jit(solution)/shard_map/jit(cholesky)/cholesky | solution.py:20
  400.0 19.7 %custom-call.24 = f32[2,128,128]{1,2,0:T(8,128)S(1)} custom-call(f32[2,128,128]{2,1,0:T(8,128)S(1)} %get-tuple-element.37), custom_call_target="InvertDiagBlocksLowerTriangular" | custom-call | tf_op jit(solution)/shard_map/triangular_solve/custom-call.0 | solution.py:22
  437.3 308.5 %all-reduce.4.cloned.1.call-done = (f32[512,256]{0,1:T(8,128)}, f32[512,256]{0,1:T(8,128)}, f32[512,256]{0,1:T(8,128)}, f32[512,256]{0,1:T(8,128)}) async-done(((f32[512,256]{0,1:T(8,128)}, f32[512,256]{0,1:T(8,128)}, f32[512,256]{0,1:T(8,128)}, f32[512,256]{0,1:T(8,128)}), (f32[512,256]{0,1:T(8,128)}, f32[512,256]{0,1:T(8,128)}, f32[512,256]{0,1:T(8,128)}, ...) | async-done | bytes 2097168 | tf_op jit(solution)/shard_map/psum | solution.py:15
  745.8 8.1 convolution_subtract_fusion.3
  756.6 17.6 %collective-permute-done.1 = f32[128,3072]{1,0:T(8,128)S(1)} collective-permute-done((f32[128,3072]{1,0:T(8,128)S(1)}, f32[128,3072]{1,0:T(8,128)S(1)}, u32[]{:S(2)}, u32[]{:S(2)}) %collective-permute-start.1) | collective-permute-done | bytes 1572896 | tf_op jit(solution)/shard_map/ppermute | solution.py:10
  788.4 18.3 %collective-permute-done.2 = f32[128,3072]{1,0:T(8,128)S(1)} collective-permute-done((f32[128,3072]{1,0:T(8,128)S(1)}, f32[128,3072]{1,0:T(8,128)S(1)}, u32[]{:S(2)}, u32[]{:S(2)}) %collective-permute-start.2) | collective-permute-done | bytes 1572896 | tf_op jit(solution)/shard_map/ppermute | solution.py:10
  810.8 7.3 convolution_subtract_fusion.1
  818.2 24.5 %collective-permute-start.3 = (f32[128,3072]{1,0:T(8,128)S(1)}, f32[128,3072]{1,0:T(8,128)S(1)}, u32[]{:S(2)}, u32[]{:S(2)}) collective-permute-start(f32[128,3072]{1,0:T(8,128)S(1)} %slice.182), channel_id=1, source_target_pairs={{0,32},{32,0},{64,96},{96,64},{1,33},{33,1},{65,97},{97,65},{2,34}... | collective-permute-start | bytes 4718600 | tf_op jit(solution)/shard_map/ppermute | solution.py:10
  849.8 9.0 %convolution_subtract_fusion = f32[512,3072]{1,0:T(8,128)} fusion(f32[512,3072]{1,0:T(8,128)} %fusion.12, f32[512,256]{0,1:T(8,128)S(1)} %copy-done.7, f32[256,3072]{1,0:T(8,128)S(1)} %copy-done.6), kind=kOutput, calls=%fused_computation.12 | convolution fusion | flops 4833411072 | bytes 16252928 | tf_op jit(solution)/shard_map/dot_general | solution.py:66
  (159 shorter events, 129.8 us)
Async XLA Ops:
  6.5 6.3 copy-start.10
  6.5 141.0 %all-gather.2.cloned.1.call-start = ((), (), s32[]{:S(2)}) async-start(), calls=%async_computation | async-start | bytes 1081344 | tf_op jit(solution)/shard_map/all_gather | solution.py:45
  13.4 732.4 %all-reduce.4.cloned.1.call-start = ((), (), s32[]{:S(2)}) async-start(), calls=%async_computation.1 | async-start | bytes 4194304 | tf_op jit(solution)/shard_map/psum | solution.py:15
  16.2 417.1 %collective-permute-start = (f32[128,3072]{1,0:T(8,128)}, f32[128,3072]{1,0:T(8,128)S(1)}, u32[]{:S(2)}, u32[]{:S(2)}) collective-permute-start(f32[128,3072]{1,0:T(8,128)} %slice.90), channel_id=1, source_target_pairs={{0,16},{1,17},{2,18},{3,19},{4,20},{5,21},{6,22},{7,23},{8,24},{9,... | collective-permute-start | bytes 4718600 | tf_op jit(solution)/shard_map/ppermute | solution.py:10
  425.4 6.8 copy-start.5
  425.4 7.9 copy-start.11
  753.9 2.7 copy-start.1
  754.0 20.2 %collective-permute-start.1 = (f32[128,3072]{1,0:T(8,128)S(1)}, f32[128,3072]{1,0:T(8,128)S(1)}, u32[]{:S(2)}, u32[]{:S(2)}) collective-permute-start(f32[128,3072]{1,0:T(8,128)S(1)} %slice.172), channel_id=1, source_target_pairs={{0,1},{1,0},{2,3},{3,2},{4,5},{5,4},{6,7},{7,6},{8,9},{9,8},{10,11... | collective-permute-start | bytes 4718600 | tf_op jit(solution)/shard_map/ppermute | solution.py:10
  775.4 3.0 copy-start.3
  775.4 2.9 copy-start.9
  785.6 2.7 copy-start.2
  785.8 20.9 %collective-permute-start.2 = (f32[128,3072]{1,0:T(8,128)S(1)}, f32[128,3072]{1,0:T(8,128)S(1)}, u32[]{:S(2)}, u32[]{:S(2)}) collective-permute-start(f32[128,3072]{1,0:T(8,128)S(1)} %slice.177), channel_id=1, source_target_pairs={{0,64},{32,96},{64,0},{96,32},{1,65},{33,97},{65,1},{97,33},{2,66}... | collective-permute-start | bytes 4718600 | tf_op jit(solution)/shard_map/ppermute | solution.py:10
  807.8 3.0 copy-start.4
  807.8 2.9 copy-start.8
  818.1 24.6 %copy-start = (f32[512,3072]{1,0:T(8,128)}, f32[512,3072]{1,0:T(8,128)S(1)}, u32[]{:S(2)}) copy-start(f32[512,3072]{1,0:T(8,128)S(1)} %convolution_subtract_fusion.1) | copy-start | bytes 18874372
  818.2 27.5 %collective-permute-start.3 = (f32[128,3072]{1,0:T(8,128)S(1)}, f32[128,3072]{1,0:T(8,128)S(1)}, u32[]{:S(2)}, u32[]{:S(2)}) collective-permute-start(f32[128,3072]{1,0:T(8,128)S(1)} %slice.182), channel_id=1, source_target_pairs={{0,32},{32,0},{64,96},{96,64},{1,33},{33,1},{65,97},{97,65},{2,34}... | collective-permute-start | bytes 4718600 | tf_op jit(solution)/shard_map/ppermute | solution.py:10
  846.9 3.0 copy-start.6
  846.9 2.9 copy-start.7
Sparse Core Ops, SparseCore 0:
  13.5 133.9 all-gather.1
  433.4 312.3 all-reduce.3
where the time goes:
time: 877 us; the launch traced here: 866 us
  waiting for transfers between devices  474 us (54%)
  other arithmetic  240 us (27%)
  matrix products  61 us (7%)
  local copies, waits for them, and re-layouts  38.9 us (4%)
  starting transfers between devices  32.4 us (4%)
  between operations  19.6 us (2%)
    psum x1, waiting for transfers between devices, broadcast(): return lax.psum(block, axis)  308 us
    another operation x28, other arithmetic, inverse_factor(): lower_factor = jnp.linalg.cholesky(symmetric)  139 us
    all_gather x1, waiting for transfers between devices, body(): whole_diagonal = lax.all_gather(diagonal_blocks, 'fc', axis=2, tiled=True)  127 us
    another operation x9, other arithmetic, inverse_factor(): lax.linalg.triangular_solve(lower_factor, identity, left_side=True, lower...  79.7 us
    ppermute x4, waiting for transfers between devices, partner(): lax.ppermute(x, axis, [(i, i ^ 1 << distance) for i in range(lax.axis_siz...  38.9 us
    ppermute x4, starting transfers between devices, partner(): lax.ppermute(x, axis, [(i, i ^ 1 << distance) for i in range(lax.axis_siz...  32.3 us
    dot_general x4, matrix products, body(): jnp.dot(slab_factor, column_factor.T, precision=HIGHEST)  31.7 us
    dot_general x4, matrix products, body(): column_factor = jnp.dot(panel_level, inverse.T, precision=HIGHEST)  23.9 us
  transfers between devices with their start and end apart: 6, of which 5 were waited for; matrix products, arithmetic and copies ran while one was open for 33% of the time, Pallas kernels for 0%

commit v1 on v0

v1 whole, which is shorter than its diff:
```python
import functools

import jax
import jax.numpy as jnp
from jax import lax
from jax.experimental import pallas as pl
from jax.experimental.pallas import tpu as pltpu
from jax.sharding import PartitionSpec as P

BF16, F32 = jnp.bfloat16, jnp.float32

def split3(x):
    hi = x.astype(BF16)
    rest = x - hi.astype(F32)
    mid = rest.astype(BF16)
    low = (rest - mid.astype(F32)).astype(BF16)
    return hi, mid, low

def dot_nt(a, b):
    return lax.dot_general(a, b, (((1,), (1,)), ((), ())), preferred_element_type=F32)

def product_nt(a, b):
    ah, am, al = split3(a)
    bh, bm, bl = split3(b)
    cat = lambda x, y: jnp.concatenate([x, y], axis=1)
    small = dot_nt(cat(am, ah), cat(bm, bl)) + dot_nt(cat(al, am), cat(bh, bh))
    return dot_nt(cat(ah, ah), cat(bh, bm)) + small

def sweep_block(block, width):
    rows, lanes = block.shape
    row = lax.broadcasted_iota(jnp.int32, (rows, lanes), 0)
    lane = lax.broadcasted_iota(jnp.int32, (rows, lanes), 1)
    own = lane % width
    group = lane - own
    own1 = own[:1]
    for p in range(0, rows, 2):
        c0 = jnp.take_along_axis(block, group + p, axis=1)
        c1 = jnp.take_along_axis(block, group + (p + 1), axis=1)
        d00, d01, d11 = c0[p:p + 1], c0[p + 1:p + 2], c1[p + 1:p + 2]
        r0 = jnp.where(own1 == p, -1.0, jnp.where(own1 == p + 1, 0.0, block[p:p + 1]))
        r1 = jnp.where(own1 == p + 1, -1.0, jnp.where(own1 == p, 0.0, block[p + 1:p + 2]))
        scale = 1.0 / (d00 * d11 - d01 * d01)
        u0 = (d11 * r0 - d01 * r1) * scale
        u1 = (d00 * r1 - d01 * r0) * scale
        at0, at1 = row == p, row == p + 1
        c0 = jnp.where(at0, -1.0, jnp.where(at1, 0.0, c0))
        c1 = jnp.where(at1, -1.0, jnp.where(at0, 0.0, c1))
        pivot = at0 | at1 | (own == p) | (own == p + 1)
        block = jnp.where(pivot, 0.0, block) - c0 * u0 - c1 * u1
    return block

def inverse_kernel(gathered_ref, inverse_ref, packed_ref, *, width):
    levels, order = inverse_ref.shape[0], inverse_ref.shape[1]
    lanes = levels * width
    blocks = order // width
    per_tile = lanes // width
    lane_group = lax.broadcasted_iota(jnp.int32, (order, lanes), 1) // width
    for level in range(levels):
        rows = gathered_ref[:, level].reshape(order, order)
        symmetric = 0.5 * (rows + rows.T)
        for b in range(blocks):
            tile, place = divmod(b, per_tile)
            piece = symmetric[:, tile * lanes:(tile + 1) * lanes]
            shift = (level - place) * width % lanes
            if shift:
                piece = pltpu.roll(piece, shift, 1)
            cols = slice(b * lanes, (b + 1) * lanes)
            if level == 0:
                packed_ref[:, cols] = piece
            else:
                packed_ref[:, cols] = jnp.where(lane_group == level, piece, packed_ref[:, cols])
    same = (lax.broadcasted_iota(jnp.int32, (lanes, lanes), 0) // width
            == lax.broadcasted_iota(jnp.int32, (lanes, lanes), 1) // width)
    small_row = lax.broadcasted_iota(jnp.int32, (width, lanes), 0)
    small_own = lax.broadcasted_iota(jnp.int32, (width, lanes), 1) % width
    minus_identity = jnp.where(small_row == small_own, -1.0, 0.0)

    def spread(x):
        return jnp.where(same, jnp.concatenate([x] * levels, axis=0), 0.0)

    def step(b, carry):
        cols = pl.ds(pl.multiple_of(b * lanes, lanes), lanes)
        rows = pl.ds(pl.multiple_of(b * width, width), width)
        negated = sweep_block(packed_ref[rows, cols], width)
        packed_ref[rows, :] = jnp.zeros((width, blocks * lanes), F32)
        packed_ref[rows, cols] = minus_identity
        column = packed_ref[:, cols]
        packed_ref[:, cols] = jnp.zeros((order, lanes), F32)
        scaled = product_nt(column, spread(negated))
        wide = jnp.concatenate(
            [spread(column[i * width:(i + 1) * width]) for i in range(blocks)], axis=0)
        packed_ref[...] += product_nt(scaled, wide)
        return carry

    lax.fori_loop(0, blocks, step, 0)
    for level in range(levels):
        for tile in range(order // lanes):
            total = None
            for place in range(per_tile):
                b = tile * per_tile + place
                piece = packed_ref[:, b * lanes:(b + 1) * lanes]
                shift = (place - level) * width % lanes
                if shift:
                    piece = pltpu.roll(piece, shift, 1)
                total = piece if total is None else jnp.where(lane_group == place, piece, total)
            inverse_ref[level, :, tile * lanes:(tile + 1) * lanes] = -total

def inverses(gathered):
    parts, levels, eight, order = gathered.shape
    width = 32
    return pl.pallas_call(
        functools.partial(inverse_kernel, width=width),
        out_shape=jax.ShapeDtypeStruct((levels, order, order), F32),
        in_specs=[pl.BlockSpec(memory_space=pltpu.VMEM)],
        out_specs=pl.BlockSpec(memory_space=pltpu.VMEM),
        scratch_shapes=[pltpu.VMEM((order, levels * order), F32)],
        compiler_params=pltpu.CompilerParams(vmem_limit_bytes=40 << 20),
        name="symmetric_inverses",
    )(gathered)


def rows_kernel(tops_ref, window_ref, inverse_ref, high_ref, low_ref, other_high_ref, other_low_ref):
    level = pl.program_id(0)
    top = tops_ref.shape[1]

    def product(x):
        y = product_nt(x, inverse_ref[0])
        high = y.astype(BF16)
        return high, (y - high.astype(F32)).astype(BF16)

    rows = jnp.concatenate([tops_ref[level], window_ref[0, top:]], axis=0)
    high_ref[...], low_ref[...] = product(rows)

    @pl.when(level == 0)
    def _():
        other_high_ref[...], other_low_ref[...] = product(tops_ref[tops_ref.shape[0] - 1])


def solved_rows(tops, window, inverse):
    levels, rows, width = window.shape
    top = tops.shape[1]
    wide = jax.ShapeDtypeStruct((rows, levels * width), BF16)
    other = jax.ShapeDtypeStruct((top, width), BF16)
    return pl.pallas_call(
        rows_kernel,
        grid=(levels,),
        out_shape=(wide, wide, other, other),
        in_specs=[
            pl.BlockSpec(tops.shape, lambda l: (0, 0, 0)),
            pl.BlockSpec((1, rows, width), lambda l: (l, 0, 0)),
            pl.BlockSpec((1, width, width), lambda l: (l, 0, 0)),
        ],
        out_specs=(
            pl.BlockSpec((rows, width), lambda l: (0, l)),
            pl.BlockSpec((rows, width), lambda l: (0, l)),
            pl.BlockSpec((top, width), lambda l: (0, 0)),
            pl.BlockSpec((top, width), lambda l: (0, 0)),
        ),
        name="solved_rows",
    )(tops, window, inverse)


def update_kernel(
    core_ref, front_ref, merged_ref, panels_ref, near_ref, far_ref, high_ref, low_ref,
    other_high_ref, other_low_ref, out_ref, *, tiles,
):
    levels = panels_ref.shape[0]
    top = merged_ref.shape[0]
    half = pl.program_id(0) // (tiles // 2)

    def split2(x):
        high = x.astype(BF16)
        return high, (x - high.astype(F32)).astype(BF16)

    def product(high, low, x):
        x_high, x_low = split2(x)
        return dot_nt(high, x_high) + (dot_nt(high, x_low) + dot_nt(low, x_high))

    columns = jnp.concatenate([panels_ref[l] for l in range(levels)], axis=1)
    update = product(high_ref[...], low_ref[...], columns)
    partner = jnp.where(half == core_ref[0], near_ref[...], far_ref[...])
    partner_update = product(other_high_ref[...], other_low_ref[...], partner)
    out_ref[:top] = merged_ref[...] - (update[:top] + partner_update)
    out_ref[top:] = front_ref[top:] - update[top:]


def updated_front(core, front, merged, panels, near, far, high, low, other_high, other_low):
    rows, cols = front.shape
    top = merged.shape[0]
    levels, _, width = panels.shape
    tile = 256
    tiles = cols // tile
    whole = lambda x: pl.BlockSpec(x.shape, lambda j, core: (0, 0))
    half = pl.BlockSpec((tile, width), lambda j, core: (lax.rem(j, tiles // 2), 0))
    return pl.pallas_call(
        functools.partial(update_kernel, tiles=tiles),
        grid_spec=pltpu.PrefetchScalarGridSpec(
            num_scalar_prefetch=1,
            grid=(tiles,),
            in_specs=[
                pl.BlockSpec((rows, tile), lambda j, core: (0, j)),
                pl.BlockSpec((top, tile), lambda j, core: (0, j)),
                pl.BlockSpec((levels, tile, width), lambda j, core: (0, j, 0)),
                half,
                half,
                whole(high),
                whole(low),
                whole(other_high),
                whole(other_low),
            ],
            out_specs=pl.BlockSpec((rows, tile), lambda j, core: (0, j)),
        ),
        out_shape=jax.ShapeDtypeStruct(front.shape, F32),
        compiler_params=pltpu.CompilerParams(vmem_limit_bytes=40 << 20),
        name="updated_front",
    )(core, front, merged, panels, near, far, high, low, other_high, other_low)


def partner(x, axis, flip):
    return lax.ppermute(x, axis, [(i, i ^ flip) for i in range(lax.axis_size(axis))])


def moved(x, row_map):
    return jnp.take(x, row_map, axis=0, mode="clip")


def to_all(x, axis):
    copies = jnp.broadcast_to(x[None], (lax.axis_size(axis), *x.shape))
    return lax.all_to_all(copies, axis, 0, 0, tiled=True)


def body(front, panels, diagonal_blocks, extend_maps):
    rows, cols = front.shape
    levels, _, width = panels.shape
    top = extend_maps.shape[3]
    row_index = lax.axis_index("fr")
    row_devices, col_devices = lax.axis_size("fr"), lax.axis_size("fc")
    maps = [extend_maps[l, 0, 0] for l in range(levels)]

    gathered = to_all(jnp.swapaxes(diagonal_blocks, 1, 2), "fc")
    own = lax.dynamic_slice_in_dim(panels, row_index * rows, rows, 1)
    own = own.reshape(levels * rows, width)
    piece = lax.all_to_all(own, "fc", 0, 0, tiled=True)[:own.shape[0] // col_devices]
    window = to_all(piece, "fc").reshape(levels, rows, width)

    core = row_index % 2
    half = cols // 2
    near = partner(lax.dynamic_slice_in_dim(panels[0], core * half, half, 0), "fc", 1)
    far = partner(near, "fr", 1)

    merged = front[:top]
    flips = [("fc", col_devices // 2), ("fc", 1), ("fr", row_devices // 2), ("fr", 1)]
    for (axis, flip), row_map in zip(flips, maps):
        merged = merged + moved(partner(merged, axis, flip), row_map)

    inverse = inverses(gathered)

    first = window[:, :top]
    lefts = jnp.concatenate([first[0], first[1], moved(first[0], maps[1])], axis=1)
    lefts = lefts + moved(partner(lefts, *flips[2]), maps[2])
    lefts = jnp.concatenate([lefts, first[2]], axis=1)
    lefts = lefts + moved(partner(lefts, *flips[3]), maps[3])
    zero, one, other, two = [lefts[:, i * width:(i + 1) * width] for i in range(4)]
    tops = jnp.stack([zero, one, two, first[3], other])

    high, low, other_high, other_low = solved_rows(tops, window, inverse)
    return updated_front(
        core[None], front, merged, panels, near, far, high, low, other_high, other_low)


def solution(mesh):
    in_specs = (P("fr", "fc"), P(None, "fc", None), P(None, None, "fc"), P(None, "fr", "fc", None))
    out_specs = P("fr", "fc")
    return jax.shard_map(body, mesh=mesh, in_specs=in_specs, out_specs=out_specs, check_vma=False)
```

time: 877 us -> 269 us (0.31)
  waiting for transfers between devices: 474 us -> 134 us
  other arithmetic: 240 us -> 13.4 us
  matrix products: 61 us -> 0 us
  Pallas kernels: 0 us -> 44.9 us
  between operations: 19.6 us -> 0.25 us
    psum x1 -> x0, waiting for transfers between devices: 308 us -> none  [broadcast(): return lax.psum(block, axis)]
    another operation x37 -> x0, other arithmetic: 219 us -> none  [the longest x28 139 us: inverse_factor(): lower_factor = jnp.linalg.cholesky(symmetric)]
    all_gather x1 -> x0, waiting for transfers between devices: 127 us -> none  [body(): whole_diagonal = lax.all_gather(diagonal_blocks, 'fc', axis=2, tiled=True)]
    ppermute x4 -> x8, waiting for transfers between devices: 38.9 us -> 134 us  [partner(): lax.ppermute(x, axis, [(i, i ^ flip) for i in range(lax.axis_size(axis))])]
    dot_general x8 -> x0, matrix products: 55.6 us -> none  [the longest x4 31.7 us: body(): jnp.dot(slab_factor, column_factor.T, precision=HIGHEST)]
    pallas_call x0 -> x3, Pallas kernels: none -> 44.9 us  [the longest x1 21.3 us: inverses(): pl.pallas_call(functools.partial(inverse_kernel, width=width), out_shape=...]
    all_to_all x0 -> x3, starting transfers between devices: none -> 27 us  [the longest x2 17.1 us: to_all(): return lax.all_to_all(copies, axis, 0, 0, tiled=True)]
    ppermute x4 -> x8, starting transfers between devices: 32.3 us -> 13.7 us  [partner(): lax.ppermute(x, axis, [(i, i ^ flip) for i in range(lax.axis_size(axis))])]
  transfers between devices with their start and end apart: 6 -> 11, of which waited for: 5 -> 3; matrix products, arithmetic and copies ran while one was open for 33% -> 13% of each run, Pallas kernels for 0% -> 10%
where the time goes in v1:
time: 269 us; the launch traced here: 266 us
  waiting for transfers between devices  134 us (50%)
  Pallas kernels  44.9 us (17%)
  starting transfers between devices  40.7 us (15%)
  local copies, waits for them, and re-layouts  32.1 us (12%)
  other arithmetic  13.4 us (5%)
    ppermute x8, waiting for transfers between devices, partner(): lax.ppermute(x, axis, [(i, i ^ flip) for i in range(lax.axis_size(axis))])  134 us
    pallas_call x1, Pallas kernels, inverses(): pl.pallas_call(functools.partial(inverse_kernel, width=width), out_shape=...  21.3 us
    pallas_call x1, Pallas kernels, updated_front(): pl.pallas_call(functools.partial(update_kernel, tiles=tiles), grid_spec=p...  17.6 us
    all_to_all x2, starting transfers between devices, to_all(): return lax.all_to_all(copies, axis, 0, 0, tiled=True)  17.1 us
    gather x7, local copies, waits for them, and re-layouts, moved(): return jnp.take(x, row_map, axis=0, mode='clip')  15.2 us
    ppermute x8, starting transfers between devices, partner(): lax.ppermute(x, axis, [(i, i ^ flip) for i in range(lax.axis_size(axis))])  13.7 us
    all_to_all x1, starting transfers between devices, body(): lax.all_to_all(own, 'fc', 0, 0, tiled=True)[:own.shape[0] // col_devices]  9.94 us
    add x4, other arithmetic, body(): merged = merged + moved(partner(merged, axis, flip), row_map)  9.43 us
  transfers between devices with their start and end apart: 11, of which 3 were waited for; matrix products, arithmetic and copies ran while one was open for 13% of the time, Pallas kernels for 10%

profile of v1, /device:TPU:1, one launch (start us, length us, event | category | flops | bytes accessed | tf_op | source)
XLA Modules:
  0.0 265.7 jit_solution(6884767629541283881)
XLA Ops:
  0.0 3.0 %constant_dynamic-slice_fusion = f32[4,512,256]{2,1,0:T(8,128)} fusion(f32[4,3072,256]{2,1,0:T(8,128)} %panels_ref.1, s32[]{:T(128)S(6)} %select_n.15), kind=kLoop, calls=%fused_computation.31 | loop fusion | bytes 4194308 | tf_op jit(solution)/shard_map/dynamic_slice | solution.py:241
  3.0 9.9 %all-to-all-start = ((f32[32,64,256]{2,1,0:T(8,128)}), f32[32,64,256]{2,1,0:T(8,128)}, u32[]{:S(2)}, u32[]{:S(2)}) async-start(f32[32,64,256]{2,1,0:T(8,128)} %bitcast.6), calls=%async_computation | async-start | bytes 4194304 | tf_op jit(solution)/shard_map/all_to_all | solution.py:243
  14.5 2.7 %collective-permute-start = (f32[128,3072]{1,0:T(8,128)S(1)}, f32[128,3072]{1,0:T(8,128)S(1)}, u32[]{:S(2)}, u32[]{:S(2)}) collective-permute-start(f32[128,3072]{1,0:T(8,128)S(1)} %slice.52), channel_id=1, source_target_pairs={{0,16},{1,17},{2,18},{3,19},{4,20},{5,21},{6,22},{7,23},{8,24},{9,... | collective-permute-start | bytes 4718600 | tf_op jit(solution)/shard_map/ppermute | solution.py:220
  17.3 55.3 %collective-permute-done = f32[128,3072]{1,0:T(8,128)S(1)} collective-permute-done((f32[128,3072]{1,0:T(8,128)S(1)}, f32[128,3072]{1,0:T(8,128)S(1)}, u32[]{:S(2)}, u32[]{:S(2)}) %collective-permute-start) | collective-permute-done | bytes 1572896 | tf_op jit(solution)/shard_map/ppermute | solution.py:220
  72.6 2.2 gather_fusion
  77.3 6.4 %all-to-all-start.1 = ((f32[32,64,256]{2,1,0:T(8,128)}), f32[32,64,256]{2,1,0:T(8,128)}, u32[]{:S(2)}, u32[]{:S(2)}) async-start(f32[32,64,256]{2,1,0:T(8,128)} %broadcast_in_dim.42), calls=%async_computation.1 | async-start | bytes 4194304 | tf_op jit(solution)/shard_map/all_to_all | solution.py:229
  83.7 1.6 slice_add_fusion
  86.5 54.2 %collective-permute-done.1 = f32[128,3072]{1,0:T(8,128)S(1)} collective-permute-done((f32[128,3072]{1,0:T(8,128)S(1)}, f32[128,3072]{1,0:T(8,128)S(1)}, u32[]{:S(2)}, u32[]{:S(2)}) %collective-permute-start.1) | collective-permute-done | bytes 1572896 | tf_op jit(solution)/shard_map/ppermute | solution.py:220
  140.7 2.3 gather_fusion.1
  143.0 2.9 %add.30 = f32[128,3072]{1,0:T(8,128)} add(f32[128,3072]{1,0:T(8,128)S(1)} %slice_add_fusion, f32[128,3072]{1,0:T(8,128)} %gather_fusion.1) | non-fusion elementwise | flops 393216 | bytes 4718592 | tf_op jit(solution)/shard_map/add | solution.py:254
  145.9 2.5 collective-permute-start.2
  150.2 1.7 slice_bitcast_fusion.5
  154.4 10.7 %all-to-all-start.2 = ((f32[32,4,8,256]{3,2,1,0:T(8,128)}), f32[32,4,8,256]{3,2,1,0:T(8,128)S(1)}, u32[]{:S(2)}, u32[]{:S(2)}) async-start(f32[32,4,8,256]{3,2,1,0:T(8,128)} %broadcast_in_dim.43), calls=%async_computation.2 | async-start | bytes 2097152 | tf_op jit(solution)/shard_map/all_to_all | solution.py:229
  165.1 24.8 %collective-permute-done.6 = f32[128,768]{1,0:T(8,128)S(1)} collective-permute-done((f32[128,768]{1,0:T(8,128)S(1)}, f32[128,768]{1,0:T(8,128)S(1)}, u32[]{:S(2)}, u32[]{:S(2)}) %collective-permute-start.6) | collective-permute-done | bytes 393248 | tf_op jit(solution)/shard_map/ppermute | solution.py:220
  192.6 1.8 pad_maximum_fusion
  194.4 5.6 %collective-permute-start.7 = (f32[128,1024]{1,0:T(8,128)}, f32[128,1024]{1,0:T(8,128)S(1)}, u32[]{:S(2)}, u32[]{:S(2)}) collective-permute-start(f32[128,1024]{1,0:T(8,128)} %pad_maximum_fusion), channel_id=1, source_target_pairs={{0,32},{32,0},{64,96},{96,64},{1,33},{33,1},{65,97},{97,65},{2,34}... | collective-permute-start | bytes 1572872 | tf_op jit(solution)/shard_map/ppermute | solution.py:220
  200.0 4.3 %gather_fusion.2 = f32[128,3072]{1,0:T(8,128)} fusion(f32[128,3072]{1,0:T(8,128)} %collective-permute-done.2, s32[1024]{0:T(1024)S(1)} %pad_clamp_fusion.1), kind=kCustom, calls=%fused_computation.2 | custom fusion | bytes 3146240 | tf_op jit(solution)/shard_map/jit(_take)/gather | solution.py:224
  204.3 3.2 %add.31 = f32[128,3072]{1,0:T(8,128)} add(f32[128,3072]{1,0:T(8,128)} %add.30, f32[128,3072]{1,0:T(8,128)} %gather_fusion.2) | non-fusion elementwise | flops 393216 | bytes 4718592 | tf_op jit(solution)/shard_map/add | solution.py:254
  208.0 21.3 %symmetric_inverses.1.inverse_ref = f32[4,256,256]{2,1,0:T(8,128)S(1)} custom-call(f32[32,4,8,256]{3,2,1,0:T(8,128)S(1)} %all-to-all-done.2.gathered_ref), custom_call_target="tpu_custom_call" | custom-call | tf_op jit(solution)/shard_map/symmetric_inverses/pallas_call | solution.py:111
  234.1 5.9 %solved_rows.1 = (bf16[512,1024]{1,0:T(8,128)(2,1)}, bf16[512,1024]{1,0:T(8,128)(2,1)}, bf16[128,256]{1,0:T(8,128)(2,1)}, bf16[128,256]{1,0:T(8,128)(2,1)}) custom-call(f32[5,128,256]{2,1,0:T(8,128)} %copy-done.9, f32[4,512,256]{2,1,0:T(8,128)} %bitcast.8.window_ref, f32[4,256,256]{2,1,0:T(8,128)} %copy-done.1), custom_call_target="tpu_custom_call" | custom-call | tf_op jit(solution)/shard_map/solved_rows/pallas_call | solution.py:144
  240.0 3.3 %gather_fusion.3 = f32[128,3072]{1,0:T(8,128)S(1)} fusion(f32[128,3072]{1,0:T(8,128)} %collective-permute-done.3, s32[1024]{0:T(1024)S(1)} %pad_clamp_fusion), kind=kCustom, calls=%fused_computation.3 | custom fusion | bytes 3146240 | tf_op jit(solution)/shard_map/jit(_take)/gather | solution.py:224
  243.3 1.7 add.32.merged_ref
  245.3 2.8 %copy-done = f32[512,3072]{1,0:T(8,128)S(1)} copy-done((f32[512,3072]{1,0:T(8,128)S(1)}, f32[512,3072]{1,0:T(8,128)}, u32[]{:S(2)}) %copy-start) | copy-done | bytes 6291480
  248.1 17.6 %updated_front.1 = f32[512,3072]{1,0:T(8,128)} custom-call(s32[1]{0:T(128)} %bitcast.core_ref, f32[512,3072]{1,0:T(8,128)S(1)} %copy-done, f32[128,3072]{1,0:T(8,128)S(1)} %add.32.merged_ref, f32[4,3072,256]{2,1,0:T(8,128)} %panels_ref.1, f32[1536,256]{1,0:T(8,128)S(1)} %collective-permute-done.4.near_ref, f32[1536,256]{1,0:T(8,128)} %collective-permute-done.5.far_ref, ...), custom_call_target="tpu_custom_call" | custom-call | tf_op jit(solution)/shard_map/updated_front/pallas_call | solution.py:195
  (59 shorter events, 17.5 us)
Async XLA Ops:
  3.0 71.8 %all-to-all-start = ((f32[32,64,256]{2,1,0:T(8,128)}), f32[32,64,256]{2,1,0:T(8,128)}, u32[]{:S(2)}, u32[]{:S(2)}) async-start(f32[32,64,256]{2,1,0:T(8,128)} %bitcast.6), calls=%async_computation | async-start | bytes 4194304 | tf_op jit(solution)/shard_map/all_to_all | solution.py:243
  13.0 4.3 %copy-start.11 = (s32[4,1,1,128]{3,2,1,0:T(1,128)S(1)}, s32[4,1,1,128]{3,2,1,0:T(1,128)}, u32[]{:S(2)}) copy-start(s32[4,1,1,128]{3,2,1,0:T(1,128)} %param.7) | copy-start | bytes 6148
  14.5 58.1 %collective-permute-start = (f32[128,3072]{1,0:T(8,128)S(1)}, f32[128,3072]{1,0:T(8,128)S(1)}, u32[]{:S(2)}, u32[]{:S(2)}) collective-permute-start(f32[128,3072]{1,0:T(8,128)S(1)} %slice.52), channel_id=1, source_target_pairs={{0,16},{1,17},{2,18},{3,19},{4,20},{5,21},{6,22},{7,23},{8,24},{9,... | collective-permute-start | bytes 4718600 | tf_op jit(solution)/shard_map/ppermute | solution.py:220
  77.3 6.4 %copy-start.6 = (f32[128,3072]{1,0:T(8,128)S(1)}, f32[128,3072]{1,0:T(8,128)}, u32[]{:S(2)}) copy-start(f32[128,3072]{1,0:T(8,128)} %gather_fusion) | copy-start | bytes 4718596
  77.3 72.9 %all-to-all-start.1 = ((f32[32,64,256]{2,1,0:T(8,128)}), f32[32,64,256]{2,1,0:T(8,128)}, u32[]{:S(2)}, u32[]{:S(2)}) async-start(f32[32,64,256]{2,1,0:T(8,128)} %broadcast_in_dim.42), calls=%async_computation.1 | async-start | bytes 4194304 | tf_op jit(solution)/shard_map/all_to_all | solution.py:229
  85.2 55.5 %collective-permute-start.1 = (f32[128,3072]{1,0:T(8,128)S(1)}, f32[128,3072]{1,0:T(8,128)S(1)}, u32[]{:S(2)}, u32[]{:S(2)}) collective-permute-start(f32[128,3072]{1,0:T(8,128)S(1)} %slice_add_fusion), channel_id=1, source_target_pairs={{0,1},{1,0},{2,3},{3,2},{4,5},{5,4},{6,7},{7,6},{8,9},{9,8},{10,11... | collective-permute-start | bytes 4718600 | tf_op jit(solution)/shard_map/ppermute | solution.py:220
  143.0 5.4 %slice-start = ((f32[4,3072,256]{2,1,0:T(8,128)}), f32[1,3072,256]{2,1,0:T(8,128)S(1)}, s32[]{:S(2)}) async-start(f32[4,3072,256]{2,1,0:T(8,128)} %panels_ref.1), calls=%async_computation.3 | async-start | bytes 6291456 | tf_op jit(solution)/shard_map/slice | solution.py:248
  145.9 54.0 %collective-permute-start.2 = (f32[128,3072]{1,0:T(8,128)}, f32[128,3072]{1,0:T(8,128)}, u32[]{:S(2)}, u32[]{:S(2)}) collective-permute-start(f32[128,3072]{1,0:T(8,128)} %add.30), channel_id=1, source_target_pairs={{0,64},{32,96},{64,0},{96,32},{1,65},{33,97},{65,1},{97,33},{2,66}... | collective-permute-start | bytes 4718600 | tf_op jit(solution)/shard_map/ppermute | solution.py:220
  149.6 3.7 %copy-start.10 = (f32[4,256,8]{1,2,0:T(8,128)S(1)}, f32[4,256,8]{1,2,0:T(8,128)}, u32[]{:S(2)}) copy-start(f32[4,256,8]{1,2,0:T(8,128)} %param.6) | copy-start | bytes 98308
  149.6 57.9 %collective-permute-start.4 = (f32[1536,256]{1,0:T(8,128)}, f32[1536,256]{1,0:T(8,128)S(1)}, u32[]{:S(2)}, u32[]{:S(2)}) collective-permute-start(f32[1536,256]{1,0:T(8,128)} %dynamic-slice_bitcast_fusion), channel_id=1, source_target_pairs={{0,1},{1,0},{2,3},{3,2},{4,5},{5,4},{6,7},{7,6},{8,9},{9,8},{10,11... | collective-permute-start | bytes 4718600 | tf_op jit(solution)/shard_map/ppermute | solution.py:220
  151.9 2.5 copy-start.8
  152.7 1.7 copy-start.7
  152.7 37.2 %collective-permute-start.6 = (f32[128,768]{1,0:T(8,128)S(1)}, f32[128,768]{1,0:T(8,128)S(1)}, u32[]{:S(2)}, u32[]{:S(2)}) collective-permute-start(f32[128,768]{1,0:T(8,128)S(1)} %pad_maximum_fusion.1), channel_id=1, source_target_pairs={{0,64},{32,96},{64,0},{96,32},{1,65},{33,97},{65,1},{97,33},{2,66}... | collective-permute-start | bytes 1179656 | tf_op jit(solution)/shard_map/ppermute | solution.py:220
  154.4 53.6 %all-to-all-start.2 = ((f32[32,4,8,256]{3,2,1,0:T(8,128)}), f32[32,4,8,256]{3,2,1,0:T(8,128)S(1)}, u32[]{:S(2)}, u32[]{:S(2)}) async-start(f32[32,4,8,256]{3,2,1,0:T(8,128)} %broadcast_in_dim.43), calls=%async_computation.2 | async-start | bytes 2097152 | tf_op jit(solution)/shard_map/all_to_all | solution.py:229
  194.4 36.0 %collective-permute-start.7 = (f32[128,1024]{1,0:T(8,128)}, f32[128,1024]{1,0:T(8,128)S(1)}, u32[]{:S(2)}, u32[]{:S(2)}) collective-permute-start(f32[128,1024]{1,0:T(8,128)} %pad_maximum_fusion), channel_id=1, source_target_pairs={{0,32},{32,0},{64,96},{96,64},{1,33},{33,1},{65,97},{97,65},{2,34}... | collective-permute-start | bytes 1572872 | tf_op jit(solution)/shard_map/ppermute | solution.py:220
  207.5 32.5 %collective-permute-start.3 = (f32[128,3072]{1,0:T(8,128)}, f32[128,3072]{1,0:T(8,128)}, u32[]{:S(2)}, u32[]{:S(2)}) collective-permute-start(f32[128,3072]{1,0:T(8,128)} %add.31), channel_id=1, source_target_pairs={{0,32},{32,0},{64,96},{96,64},{1,33},{33,1},{65,97},{97,65},{2,34}... | collective-permute-start | bytes 4718600 | tf_op jit(solution)/shard_map/ppermute | solution.py:220
  207.5 37.5 %collective-permute-start.5 = (f32[1536,256]{1,0:T(8,128)S(1)}, f32[1536,256]{1,0:T(8,128)}, u32[]{:S(2)}, u32[]{:S(2)}) collective-permute-start(f32[1536,256]{1,0:T(8,128)S(1)} %collective-permute-done.4.near_ref), channel_id=1, source_target_pairs={{0,32},{32,0},{64,96},{96,64},{1,33},{33,1},{65,97},{97,65},{2,34}... | collective-permute-start | bytes 4718600 | tf_op jit(solution)/shard_map/ppermute | solution.py:220
  229.4 1.0 copy-start.1
  233.1 0.9 copy-start.9
  243.3 1.8 copy-start.2
  243.3 2.0 copy-start.3
  243.3 2.0 copy-start.4
  243.3 2.0 copy-start.5
  245.3 2.8 %copy-start = (f32[512,3072]{1,0:T(8,128)S(1)}, f32[512,3072]{1,0:T(8,128)}, u32[]{:S(2)}) copy-start(f32[512,3072]{1,0:T(8,128)} %front_ref.1) | copy-start | bytes 18874372

commit v2 on v1

--- a/solution.py
+++ b/solution.py
@@ -8,6 +8,7 @@
 from jax.sharding import PartitionSpec as P
 
 BF16, F32 = jnp.bfloat16, jnp.float32
+COST = pl.CostEstimate(flops=1, bytes_accessed=1, transcendentals=0)
 
 def split3(x):
     hi = x.astype(BF16)
@@ -114,84 +115,85 @@
         in_specs=[pl.BlockSpec(memory_space=pltpu.VMEM)],
         out_specs=pl.BlockSpec(memory_space=pltpu.VMEM),
         scratch_shapes=[pltpu.VMEM((order, levels * order), F32)],
-        compiler_params=pltpu.CompilerParams(vmem_limit_bytes=40 << 20),
+        compiler_params=pltpu.CompilerParams(vmem_limit_bytes=16 << 20),
+        cost_estimate=COST,
         name="symmetric_inverses",
     )(gathered)
 
 
-def rows_kernel(tops_ref, window_ref, inverse_ref, high_ref, low_ref, other_high_ref, other_low_ref):
-    level = pl.program_id(0)
-    top = tops_ref.shape[1]
-
-    def product(x):
-        y = product_nt(x, inverse_ref[0])
-        high = y.astype(BF16)
-        return high, (y - high.astype(F32)).astype(BF16)
-
-    rows = jnp.concatenate([tops_ref[level], window_ref[0, top:]], axis=0)
-    high_ref[...], low_ref[...] = product(rows)
-
-    @pl.when(level == 0)
+def split2(x):
+    high = x.astype(BF16)
+    return high, (x - high.astype(F32)).astype(BF16)
+
+
+def product2_nt(a, b):
+    return dot_nt(a[0], b[0]) + (dot_nt(a[0], b[1]) + dot_nt(a[1], b[0]))
+
+
+def moved(x, row_map):
+    rows = x.shape[0]
+    pick = lax.broadcasted_iota(jnp.int32, (rows, rows), 0) == row_map
+    pick = jnp.where(pick, 1.0, 0.0).T.astype(BF16)
+    high, mid, low = (jnp.dot(pick, part, preferred_element_type=F32) for part in split3(x))
+    return (high + mid) + low
+
+
+def merge_kernel(own_ref, received_ref, map_ref, out_ref):
+    step = 256
+    for start in range(0, out_ref.shape[1], step):
+        cols = slice(start, start + step)
+        out_ref[:, cols] = own_ref[:, cols] + moved(received_ref[:, cols], map_ref[...])
+
+
+def merge(own, received, row_map):
+    return pl.pallas_call(
+        merge_kernel,
+        out_shape=jax.ShapeDtypeStruct(own.shape, F32),
+        in_specs=[pl.BlockSpec(memory_space=pltpu.VMEM)] * 3,
+        out_specs=pl.BlockSpec(memory_space=pltpu.VMEM),
+        compiler_params=pltpu.CompilerParams(vmem_limit_bytes=8 << 20),
+        cost_estimate=COST,
+        name="merge",
+    )(own, received, row_map)
+
+
+def update_kernel(
+    core_ref, front_ref, panels_ref, near_ref, far_ref, lefts_ref, window_ref, inverse_ref, out_ref,
+    high_ref, low_ref, other_high_ref, other_low_ref, *, tiles,
+):
+    levels, rows, width = window_ref.shape
+    top = lefts_ref.shape[1]
+
+    @pl.when(pl.program_id(0) == 0)
     def _():
-        other_high_ref[...], other_low_ref[...] = product(tops_ref[tops_ref.shape[0] - 1])
-
-
-def solved_rows(tops, window, inverse):
-    levels, rows, width = window.shape
-    top = tops.shape[1]
-    wide = jax.ShapeDtypeStruct((rows, levels * width), BF16)
-    other = jax.ShapeDtypeStruct((top, width), BF16)
-    return pl.pallas_call(
-        rows_kernel,
-        grid=(levels,),
-        out_shape=(wide, wide, other, other),
-        in_specs=[
-            pl.BlockSpec(tops.shape, lambda l: (0, 0, 0)),
-            pl.BlockSpec((1, rows, width), lambda l: (l, 0, 0)),
-            pl.BlockSpec((1, width, width), lambda l: (l, 0, 0)),
-        ],
-        out_specs=(
-            pl.BlockSpec((rows, width), lambda l: (0, l)),
-            pl.BlockSpec((rows, width), lambda l: (0, l)),
-            pl.BlockSpec((top, width), lambda l: (0, 0)),
-            pl.BlockSpec((top, width), lambda l: (0, 0)),
-        ),
-        name="solved_rows",
-    )(tops, window, inverse)
-
-
-def update_kernel(
-    core_ref, front_ref, merged_ref, panels_ref, near_ref, far_ref, high_ref, low_ref,
-    other_high_ref, other_low_ref, out_ref, *, tiles,
-):
-    levels = panels_ref.shape[0]
-    top = merged_ref.shape[0]
+        for level in range(levels):
+            cols = slice(level * width, (level + 1) * width)
+            inverse = split2(inverse_ref[level])
+            left = jnp.concatenate([lefts_ref[level], window_ref[level, top:]], axis=0)
+            high_ref[:, cols], low_ref[:, cols] = split2(product2_nt(split2(left), inverse))
+            if level == 0:
+                solved = product2_nt(split2(lefts_ref[levels]), inverse)
+                other_high_ref[...], other_low_ref[...] = split2(solved)
+
+    columns = jnp.concatenate([panels_ref[level] for level in range(levels)], axis=1)
+    update = product2_nt((high_ref[...], low_ref[...]), split2(columns))
     half = pl.program_id(0) // (tiles // 2)
-
-    def split2(x):
-        high = x.astype(BF16)
-        return high, (x - high.astype(F32)).astype(BF16)
-
-    def product(high, low, x):
-        x_high, x_low = split2(x)
-        return dot_nt(high, x_high) + (dot_nt(high, x_low) + dot_nt(low, x_high))
-
-    columns = jnp.concatenate([panels_ref[l] for l in range(levels)], axis=1)
-    update = product(high_ref[...], low_ref[...], columns)
-    partner = jnp.where(half == core_ref[0], near_ref[...], far_ref[...])
-    partner_update = product(other_high_ref[...], other_low_ref[...], partner)
-    out_ref[:top] = merged_ref[...] - (update[:top] + partner_update)
+    other = jnp.where(half == core_ref[0], near_ref[...], far_ref[...])
+    other = product2_nt((other_high_ref[...], other_low_ref[...]), split2(other))
+    out_ref[:top] = -update[:top] - other
     out_ref[top:] = front_ref[top:] - update[top:]
 
 
-def updated_front(core, front, merged, panels, near, far, high, low, other_high, other_low):
+def updated_rows(core, front, panels, near, far, lefts, window, inverse):
     rows, cols = front.shape
-    top = merged.shape[0]
+    top = lefts.shape[1]
     levels, _, width = panels.shape
     tile = 256
     tiles = cols // tile
-    whole = lambda x: pl.BlockSpec(x.shape, lambda j, core: (0, 0))
+    whole = lambda x: pl.BlockSpec(x.shape, lambda j, core: (0,) * x.ndim)
     half = pl.BlockSpec((tile, width), lambda j, core: (lax.rem(j, tiles // 2), 0))
+    wide = pltpu.VMEM((rows, levels * width), BF16)
+    other = pltpu.VMEM((top, width), BF16)
     return pl.pallas_call(
         functools.partial(update_kernel, tiles=tiles),
         grid_spec=pltpu.PrefetchScalarGridSpec(
@@ -199,34 +201,109 @@
             grid=(tiles,),
             in_specs=[
                 pl.BlockSpec((rows, tile), lambda j, core: (0, j)),
-                pl.BlockSpec((top, tile), lambda j, core: (0, j)),
                 pl.BlockSpec((levels, tile, width), lambda j, core: (0, j, 0)),
                 half,
                 half,
-                whole(high),
-                whole(low),
-                whole(other_high),
-                whole(other_low),
+                whole(lefts),
+                whole(window),
+                whole(inverse),
             ],
             out_specs=pl.BlockSpec((rows, tile), lambda j, core: (0, j)),
+            scratch_shapes=[wide, wide, other, other],
         ),
         out_shape=jax.ShapeDtypeStruct(front.shape, F32),
-        compiler_params=pltpu.CompilerParams(vmem_limit_bytes=40 << 20),
-        name="updated_front",
-    )(core, front, merged, panels, near, far, high, low, other_high, other_low)
+        compiler_params=pltpu.CompilerParams(vmem_limit_bytes=24 << 20),
+        cost_estimate=COST,
+        name="updated_rows",
+    )(core, front, panels, near, far, lefts, window, inverse)
+
+
+def finish_kernel(own_ref, received_ref, map_ref, rest_ref, out_ref):
+    out_ref[...] = own_ref[...] + moved(received_ref[...], map_ref[...]) + rest_ref[...]
+
+
+def finished(own, received, row_map, updated, part):
+    rows, cols = own.shape
+    steps = 2
+    tile = cols // steps
+    block = pl.BlockSpec((rows, tile), lambda j: (0, j))
+    placed = pl.BlockSpec((rows, tile), lambda j: (0, part * steps + j))
+    return pl.pallas_call(
+        finish_kernel,
+        grid=(steps,),
+        in_specs=[block, block, pl.BlockSpec((1, rows), lambda j: (0, 0)), placed],
+        out_specs=placed,
+        out_shape=jax.ShapeDtypeStruct(updated.shape, F32),
+        input_output_aliases={3: 0},
+        compiler_params=pltpu.CompilerParams(vmem_limit_bytes=8 << 20),
+        cost_estimate=COST,
+        name="finished",
+    )(own, received, row_map, updated)
 
 
 def partner(x, axis, flip):
     return lax.ppermute(x, axis, [(i, i ^ flip) for i in range(lax.axis_size(axis))])
 
 
-def moved(x, row_map):
-    return jnp.take(x, row_map, axis=0, mode="clip")
-
-
-def to_all(x, axis):
-    copies = jnp.broadcast_to(x[None], (lax.axis_size(axis), *x.shape))
-    return lax.all_to_all(copies, axis, 0, 0, tiled=True)
+def after(x, *earlier):
+    return lax.optimization_barrier((x, *earlier))[0]
+
+
+def to_all(x, axis, flips=None):
+    if flips is None:
+        flips = [1 << bit for bit in range(lax.axis_size(axis).bit_length() - 1)]
+    groups = []
+    for start in range(lax.axis_size(axis)):
+        group = [start]
+        for flip in flips:
+            group += [index ^ flip for index in group]
+        if start == min(group):
+            groups.append(sorted(group))
+    copies = jnp.broadcast_to(x[None], (len(groups[0]), *x.shape))
+    return lax.all_to_all(copies, axis, 0, 0, tiled=True, axis_index_groups=groups)
+
+
+def dealt(parts, axis, sizes):
+    count = parts.shape[0]
+
+    def place(index):
+        found = []
+        for size in reversed(sizes):
+            found.append(index % size)
+            index //= size
+        return found
+
+    def distance(a, b):
+        steps = [(abs(i - j), size) for i, j, size in zip(place(a), place(b), reversed(sizes))]
+        return sum(min(step, size - step) for step, size in steps)
+
+    holders = [index for index in range(count) if sum(place(index)) <= 1]
+    most = -(-count // len(holders))
+    shares = {holder: [holder] for holder in holders}
+    for index in sorted(range(count), key=lambda i: (-distance(i, 0), i)):
+        if index not in holders:
+            free = [h for h in holders if len(shares[h]) < most]
+            shares[min(free, key=lambda h: (distance(h, index), len(shares[h])))].append(index)
+    for share in shares.values():
+        share += [share[0]] * (most - len(share))
+
+    device = lax.axis_index(axis)
+    held = [
+        lax.ppermute(jnp.stack([parts[i] for i in shares[holder]]), axis, [(0, holder)])
+        for holder in holders if holder
+    ]
+
+    def rest(held):
+        first = jnp.stack([parts[i] for i in shares[0]])
+        held = jnp.where(device == 0, first, functools.reduce(jnp.add, held))
+        received = [held[0]]
+        for slot in range(1, most):
+            pairs = [(h, share[slot]) for h, share in shares.items() if share[slot] != h]
+            received.append(lax.ppermute(held[slot], axis, pairs))
+        is_holder = functools.reduce(jnp.logical_or, [device == h for h in holders])
+        return jnp.where(is_holder, received[0], functools.reduce(jnp.add, received[1:]))
+
+    return held, rest
 
 
 def body(front, panels, diagonal_blocks, extend_maps):
@@ -235,38 +312,56 @@
     top = extend_maps.shape[3]
     row_index = lax.axis_index("fr")
     row_devices, col_devices = lax.axis_size("fr"), lax.axis_size("fc")
-    maps = [extend_maps[l, 0, 0] for l in range(levels)]
-
-    gathered = to_all(jnp.swapaxes(diagonal_blocks, 1, 2), "fc")
-    own = lax.dynamic_slice_in_dim(panels, row_index * rows, rows, 1)
-    own = own.reshape(levels * rows, width)
-    piece = lax.all_to_all(own, "fc", 0, 0, tiled=True)[:own.shape[0] // col_devices]
-    window = to_all(piece, "fc").reshape(levels, rows, width)
-
+    maps = [extend_maps[l, 0] for l in range(levels)]
+    flips = [("fc", col_devices // 2), ("fc", 1), ("fr", row_devices // 2), ("fr", 1)]
     core = row_index % 2
     half = cols // 2
-    near = partner(lax.dynamic_slice_in_dim(panels[0], core * half, half, 0), "fc", 1)
+
+    own_a, own_b = front[:top, :half], front[:top, half:]
+    received_a = partner(own_a, *flips[0])
+
+    own = lax.dynamic_slice_in_dim(panels, row_index * rows, rows, 1)
+    held, rest = dealt(own.reshape(col_devices, -1, width), "fc", (4, 2, 4))
+    near = lax.dynamic_slice_in_dim(panels[0], core * half, half, 0)
+    near = partner(near, "fc", 1)
+    gathered = to_all(jnp.swapaxes(diagonal_blocks, 1, 2), "fc")
+
+    merged_a = merge(own_a, received_a, maps[0])
+    received_a = partner(merged_a, *flips[1])
+    received_b = partner(after(own_b, merged_a), *flips[0])
+    part = rest(after(held, merged_a))
+    part = to_all(part, "fc", [1, 2, 4])
+    window = to_all(part, "fc", [8, 16])
+    inverse = inverses(after(gathered, part, merged_a))
     far = partner(near, "fr", 1)
 
-    merged = front[:top]
-    flips = [("fc", col_devices // 2), ("fc", 1), ("fr", row_devices // 2), ("fr", 1)]
-    for (axis, flip), row_map in zip(flips, maps):
-        merged = merged + moved(partner(merged, axis, flip), row_map)
-
-    inverse = inverses(gathered)
-
+    merged_b = merge(own_b, after(received_b, inverse), maps[0])
+    merged_a = merge(merged_a, after(received_a, inverse), maps[1])
+    received_b = partner(merged_b, *flips[1])
+    received_a = partner(merged_a, *flips[2])
+
+    window = after(window, merged_a, merged_b).reshape(levels, rows, width)
     first = window[:, :top]
-    lefts = jnp.concatenate([first[0], first[1], moved(first[0], maps[1])], axis=1)
-    lefts = lefts + moved(partner(lefts, *flips[2]), maps[2])
+    turned = jnp.take(first[0], maps[1][0], axis=0, mode="clip")
+    lefts = jnp.concatenate([first[0], first[1], turned], axis=1)
+    lefts = merge(lefts, partner(lefts, *flips[2]), maps[2])
     lefts = jnp.concatenate([lefts, first[2]], axis=1)
-    lefts = lefts + moved(partner(lefts, *flips[3]), maps[3])
+    lefts = merge(lefts, partner(lefts, *flips[3]), maps[3])
     zero, one, other, two = [lefts[:, i * width:(i + 1) * width] for i in range(4)]
-    tops = jnp.stack([zero, one, two, first[3], other])
-
-    high, low, other_high, other_low = solved_rows(tops, window, inverse)
-    return updated_front(
-        core[None], front, merged, panels, near, far, high, low, other_high, other_low)
-
+    lefts = jnp.stack([zero, one, two, first[3], other])
+
+    merged_b = merge(merged_b, received_b, maps[1])
+    merged_a = merge(merged_a, received_a, maps[2])
+    received_b = partner(merged_b, *flips[2])
+    received_a = partner(merged_a, *flips[3])
+
+    updated = updated_rows(
+        core[None], front, panels, near, far, after(lefts, merged_a, merged_b), window, inverse)
+
+    merged_b = merge(merged_b, after(received_b, updated), maps[2])
+    received_b = partner(merged_b, *flips[3])
+    updated = finished(merged_a, received_a, maps[3], updated, 0)
+    return finished(merged_b, received_b, maps[3], updated, 1)
 
 def solution(mesh):
     in_specs = (P("fr", "fc"), P(None, "fc", None), P(None, None, "fc"), P(None, "fr", "fc", None))

time: 269 us -> 185 us (0.69)
  waiting for transfers between devices: 134 us -> 34 us
  starting transfers between devices: 40.7 us -> 60.1 us
  blocking collectives: 0 us -> 11.1 us
  other arithmetic: 13.4 us -> 2.51 us
  local copies, waits for them, and re-layouts: 32.1 us -> 25.9 us
  Pallas kernels: 44.9 us -> 49.2 us
    ppermute x8 -> x12, waiting for transfers between devices: 134 us -> 22.5 us  [partner(): lax.ppermute(x, axis, [(i, i ^ flip) for i in range(lax.axis_size(axis))])]
    ppermute x8 -> x12, starting transfers between devices: 13.7 us -> 32.4 us  [partner(): lax.ppermute(x, axis, [(i, i ^ flip) for i in range(lax.axis_size(axis))])]
    ppermute x0 -> x10, starting transfers between devices: none -> 17.1 us  [the longest x7 9.05 us: rest(): received.append(lax.ppermute(held[slot], axis, pairs))]
    all_to_all x3 -> x2, starting transfers between devices: 27 us -> 10.5 us  [to_all(): lax.all_to_all(copies, axis, 0, 0, tiled=True, axis_index_groups=groups)]
    gather x7 -> x1, local copies, waits for them, and re-layouts: 15.2 us -> 0.75 us  [body(): turned = jnp.take(first[0], maps[1][0], axis=0, mode='clip')]
    add x6 -> x0, other arithmetic: 11.5 us -> none  [the longest x4 9.43 us: body(): merged = merged + moved(partner(merged, axis, flip), row_map)]
    ppermute x0 -> x10, waiting for transfers between devices: none -> 11.5 us  [the longest x3 10.2 us: dealt(): lax.ppermute(jnp.stack([parts[i] for i in shares[holder]]), axis, [(0, ho...]
    all_to_all x0 -> x1, blocking collectives: none -> 11.1 us  [to_all(): lax.all_to_all(copies, axis, 0, 0, tiled=True, axis_index_groups=groups)]
  transfers between devices with their start and end apart: 11 -> 24, of which waited for: 3 -> 7; matrix products, arithmetic and copies ran while one was open for 13% -> 9% of each run, Pallas kernels for 10% -> 25%
where the time goes in v2:
time: 185 us; the launch traced here: 183 us
  starting transfers between devices  60.1 us (32%)
  Pallas kernels  49.2 us (27%)
  waiting for transfers between devices  34 us (18%)
  local copies, waits for them, and re-layouts  25.9 us (14%)
  blocking collectives  11.1 us (6%)
  other arithmetic  2.51 us (1%)
    ppermute x12, starting transfers between devices, partner(): lax.ppermute(x, axis, [(i, i ^ flip) for i in range(lax.axis_size(axis))])  32.4 us
    ppermute x12, waiting for transfers between devices, partner(): lax.ppermute(x, axis, [(i, i ^ flip) for i in range(lax.axis_size(axis))])  22.5 us
    pallas_call x1, Pallas kernels, inverses(): pl.pallas_call(functools.partial(inverse_kernel, width=width), out_shape=...  21.4 us
    pallas_call x1, Pallas kernels, updated_rows(): pl.pallas_call(functools.partial(update_kernel, tiles=tiles), grid_spec=p...  18.7 us
    unnamed x43, local copies, waits for them, and re-layouts  13.7 us
    all_to_all x1, blocking collectives, to_all(): lax.all_to_all(copies, axis, 0, 0, tiled=True, axis_index_groups=groups)  11.1 us
    all_to_all x2, starting transfers between devices, to_all(): lax.all_to_all(copies, axis, 0, 0, tiled=True, axis_index_groups=groups)  10.5 us
    ppermute x3, waiting for transfers between devices, dealt(): lax.ppermute(jnp.stack([parts[i] for i in shares[holder]]), axis, [(0, ho...  10.2 us
  transfers between devices with their start and end apart: 24, of which 7 were waited for; matrix products, arithmetic and copies ran while one was open for 9% of the time, Pallas kernels for 25%

profile of v2, /device:TPU:1, one launch (start us, length us, event | category | flops | bytes accessed | tf_op | source)
XLA Modules:
  0.0 183.2 jit_solution(8430895696947511411)
XLA Ops:
  0.0 2.4 %fusion.5 = (f32[128,1536]{1,0:T(8,128)S(1)}, f32[128,1536]{1,0:T(8,128)}) fusion(f32[512,3072]{1,0:T(8,128)} %front_ref.1), kind=kLoop, calls=%fused_computation.63 | loop fusion | bytes 3145728 | tf_op jit(solution)/shard_map/slice | solution.py:320
  2.4 4.4 %collective-permute-start = (f32[128,1536]{1,0:T(8,128)S(1)}, f32[128,1536]{1,0:T(8,128)S(1)}, u32[]{:S(2)}, u32[]{:S(2)}) collective-permute-start(f32[128,1536]{1,0:T(8,128)S(1)} %get-tuple-element.25.own_ref), channel_id=1, source_target_pairs={{0,16},{1,17},{2,18},{3,19},{4,20},{5,21},{6,22},{7,23},{8,24},{9,... | collective-permute-start | bytes 2359304 | tf_op jit(solution)/shard_map/ppermute | solution.py:245
  7.9 6.0 %all-to-all-start = ((f32[32,4,8,256]{3,2,1,0:T(8,128)}), f32[32,4,8,256]{3,2,1,0:T(8,128)S(1)}, u32[]{:S(2)}, u32[]{:S(2)}) async-start(f32[32,4,8,256]{3,2,1,0:T(8,128)} %broadcast_in_dim.11), calls=%async_computation | async-start | bytes 2097152 | tf_op jit(solution)/shard_map/all_to_all | solution.py:263
  13.9 1.7 constant_dynamic-slice_fusion
  21.1 3.9 %collective-permute-start.2 = (f32[8,64,256]{2,1,0:T(8,128)}, f32[8,64,256]{2,1,0:T(8,128)}, u32[]{:S(2)}, u32[]{:S(2)}) collective-permute-start(f32[8,64,256]{2,1,0:T(8,128)} %get-tuple-element.34), channel_id=1, source_target_pairs={{0,1},{32,33},{64,65},{96,97}} | collective-permute-start | bytes 1572872 | tf_op jit(solution)/shard_map/ppermute | solution.py:292
  25.0 2.1 %collective-permute-start.3 = (f32[8,64,256]{2,1,0:T(8,128)}, f32[8,64,256]{2,1,0:T(8,128)}, u32[]{:S(2)}, u32[]{:S(2)}) collective-permute-start(f32[8,64,256]{2,1,0:T(8,128)} %get-tuple-element.33), channel_id=1, source_target_pairs={{0,4},{32,36},{64,68},{96,100}} | collective-permute-start | bytes 1572872 | tf_op jit(solution)/shard_map/ppermute | solution.py:292
  27.8 2.1 %collective-permute-start.4 = (f32[8,64,256]{2,1,0:T(8,128)}, f32[8,64,256]{2,1,0:T(8,128)}, u32[]{:S(2)}, u32[]{:S(2)}) collective-permute-start(f32[8,64,256]{2,1,0:T(8,128)} %get-tuple-element.30), channel_id=1, source_target_pairs={{0,8},{32,40},{64,72},{96,104}} | collective-permute-start | bytes 1572872 | tf_op jit(solution)/shard_map/ppermute | solution.py:292
  30.7 3.2 %collective-permute-done.received_ref = f32[128,1536]{1,0:T(8,128)S(1)} collective-permute-done((f32[128,1536]{1,0:T(8,128)S(1)}, f32[128,1536]{1,0:T(8,128)S(1)}, u32[]{:S(2)}, u32[]{:S(2)}) %collective-permute-start) | collective-permute-done | bytes 786464 | tf_op jit(solution)/shard_map/ppermute | solution.py:245
  36.4 9.2 %collective-permute-done.4 = f32[8,64,256]{2,1,0:T(8,128)} collective-permute-done((f32[8,64,256]{2,1,0:T(8,128)}, f32[8,64,256]{2,1,0:T(8,128)}, u32[]{:S(2)}, u32[]{:S(2)}) %collective-permute-start.4) | collective-permute-done | bytes 524320 | tf_op jit(solution)/shard_map/ppermute | solution.py:292
  57.7 11.1 %all_to_all.15 = f32[8,64,256]{2,1,0:T(8,128)S(1)} all-to-all(f32[8,64,256]{2,1,0:T(8,128)S(1)} %broadcast_in_dim.12), channel_id=1, replica_groups={{0,1,2,3,4,5,6,7},{8,9,10,11,12,13,14,15},{16,17,18,19,20,21,22,23},{24..., dimensions={0} | all-to-all | bytes 1048576 | tf_op jit(solution)/shard_map/all_to_all | solution.py:263
  70.4 4.6 %all-to-all-start.2 = ((f32[4,8,64,256]{3,2,1,0:T(8,128)}), f32[4,8,64,256]{3,2,1,0:T(8,128)}, u32[]{:S(2)}, u32[]{:S(2)}) async-start(f32[4,8,64,256]{3,2,1,0:T(8,128)} %broadcast_in_dim.28), calls=%async_computation.2 | async-start | bytes 4194304 | tf_op jit(solution)/shard_map/all_to_all | solution.py:263
  75.0 3.1 %collective-permute-start.1 = (f32[128,1536]{1,0:T(8,128)}, f32[128,1536]{1,0:T(8,128)S(1)}, u32[]{:S(2)}, u32[]{:S(2)}) collective-permute-start(f32[128,1536]{1,0:T(8,128)} %get-tuple-element.15.own_ref), channel_id=1, source_target_pairs={{0,16},{1,17},{2,18},{3,19},{4,20},{5,21},{6,22},{7,23},{8,24},{9,... | collective-permute-start | bytes 2359304 | tf_op jit(solution)/shard_map/ppermute | solution.py:245
  80.9 21.4 %symmetric_inverses.1.inverse_ref = f32[4,256,256]{2,1,0:T(8,128)S(1)} custom-call(f32[32,4,8,256]{3,2,1,0:T(8,128)S(1)} %copy-done.2), custom_call_target="tpu_custom_call" | custom-call | flops 1 | bytes 1 | tf_op jit(solution)/shard_map/symmetric_inverses/pallas_call | solution.py:112
  102.2 11.8 %collective-permute-done.1.received_ref = f32[128,1536]{1,0:T(8,128)S(1)} collective-permute-done((f32[128,1536]{1,0:T(8,128)}, f32[128,1536]{1,0:T(8,128)S(1)}, u32[]{:S(2)}, u32[]{:S(2)}) %collective-permute-start.1) | collective-permute-done | bytes 786464 | tf_op jit(solution)/shard_map/ppermute | solution.py:245
  116.9 1.7 slice_bitcast_fusion.5
  119.4 2.8 %collective-permute-start.17 = (f32[128,768]{1,0:T(8,128)S(1)}, f32[128,768]{1,0:T(8,128)S(1)}, u32[]{:S(2)}, u32[]{:S(2)}) collective-permute-start(f32[128,768]{1,0:T(8,128)S(1)} %pad_maximum_fusion.1.own_ref), channel_id=1, source_target_pairs={{0,64},{32,96},{64,0},{96,32},{1,65},{33,97},{65,1},{97,33},{2,66}... | collective-permute-start | bytes 1179656 | tf_op jit(solution)/shard_map/ppermute | solution.py:245
  122.4 5.2 %collective-permute-done.17.received_ref = f32[128,768]{1,0:T(8,128)S(1)} collective-permute-done((f32[128,768]{1,0:T(8,128)S(1)}, f32[128,768]{1,0:T(8,128)S(1)}, u32[]{:S(2)}, u32[]{:S(2)}) %collective-permute-start.17) | collective-permute-done | bytes 393248 | tf_op jit(solution)/shard_map/ppermute | solution.py:245
  128.9 10.6 %collective-permute-start.18 = (f32[128,1024]{1,0:T(8,128)S(1)}, f32[128,1024]{1,0:T(8,128)S(1)}, u32[]{:S(2)}, u32[]{:S(2)}) collective-permute-start(f32[128,1024]{1,0:T(8,128)S(1)} %pad_maximum_fusion.own_ref), channel_id=1, source_target_pairs={{0,32},{32,0},{64,96},{96,64},{1,33},{33,1},{65,97},{97,65},{2,34}... | collective-permute-start | bytes 1572872 | tf_op jit(solution)/shard_map/ppermute | solution.py:245
  139.7 2.4 %collective-permute-done.12.received_ref = f32[128,1536]{1,0:T(8,128)S(1)} collective-permute-done((f32[128,1536]{1,0:T(8,128)}, f32[128,1536]{1,0:T(8,128)S(1)}, u32[]{:S(2)}, u32[]{:S(2)}) %collective-permute-start.12) | collective-permute-done | bytes 786464 | tf_op jit(solution)/shard_map/ppermute | solution.py:245
  144.6 8.1 %collective-permute-start.21 = (f32[128,1536]{1,0:T(8,128)S(1)}, f32[128,1536]{1,0:T(8,128)S(1)}, u32[]{:S(2)}, u32[]{:S(2)}) collective-permute-start(f32[128,1536]{1,0:T(8,128)S(1)} %merge.14.own_ref), channel_id=1, source_target_pairs={{0,32},{32,0},{64,96},{96,64},{1,33},{33,1},{65,97},{97,65},{2,34}... | collective-permute-start | bytes 2359304 | tf_op jit(solution)/shard_map/ppermute | solution.py:245
  154.1 4.6 %copy-done = f32[4,3072,256]{2,1,0:T(8,128)S(1)} copy-done((f32[4,3072,256]{2,1,0:T(8,128)S(1)}, f32[4,3072,256]{2,1,0:T(8,128)}, u32[]{:S(2)}) %copy-start) | copy-done | bytes 12582936
  158.7 18.7 %updated_rows.1.rest_ref = f32[512,3072]{1,0:T(8,128)} custom-call(s32[1]{0:T(128)} %bitcast.12.core_ref, f32[512,3072]{1,0:T(8,128)S(1)} %bitcast.57, f32[4,3072,256]{2,1,0:T(8,128)S(1)} %copy-done, f32[1536,256]{1,0:T(8,128)} %collective-permute-done.14.near_ref, f32[1536,256]{1,0:T(8,128)S(1)} %collective-permute-done.15.far_ref, ...), custom_call_target="tpu_custom_call" | custom-call | flops 1 | bytes 1 | tf_op jit(solution)/shard_map/updated_rows/pallas_call | solution.py:197
  178.1 2.6 %finished.2.rest_ref = f32[512,3072]{1,0:T(8,128)} custom-call(f32[128,1536]{1,0:T(8,128)S(1)} %merge.14.own_ref, f32[128,1536]{1,0:T(8,128)S(1)} %collective-permute-done.21.received_ref, s32[1,128]{1,0:T(1,128)S(1)} %get-tuple-element.65.map_ref, f32[512,3072]{1,0:T(8,128)} %updated_rows.1.rest_ref), custom_call_target="tpu_custom_call", output_to_operand_aliasing={{}: (3, {})} | custom-call | flops 1 | bytes 1 | tf_op jit(solution)/shard_map/finished/pallas_call | solution.py:231
  180.6 2.6 %finished.3 = f32[512,3072]{1,0:T(8,128)} custom-call(f32[128,1536]{1,0:T(8,128)S(1)} %merge.15.own_ref, f32[128,1536]{1,0:T(8,128)S(1)} %collective-permute-done.20.received_ref, s32[1,128]{1,0:T(1,128)S(1)} %get-tuple-element.65.map_ref, f32[512,3072]{1,0:T(8,128)} %finished.2.rest_ref), custom_call_target="tpu_custom_call", output_to_operand_aliasing={{}: (3, {})} | custom-call | flops 1 | bytes 1 | tf_op jit(solution)/shard_map/finished/pallas_call | solution.py:231
  (101 shorter events, 36.6 us)
Async XLA Ops:
  2.4 31.6 %collective-permute-start = (f32[128,1536]{1,0:T(8,128)S(1)}, f32[128,1536]{1,0:T(8,128)S(1)}, u32[]{:S(2)}, u32[]{:S(2)}) collective-permute-start(f32[128,1536]{1,0:T(8,128)S(1)} %get-tuple-element.25.own_ref), channel_id=1, source_target_pairs={{0,16},{1,17},{2,18},{3,19},{4,20},{5,21},{6,22},{7,23},{8,24},{9,... | collective-permute-start | bytes 2359304 | tf_op jit(solution)/shard_map/ppermute | solution.py:245
  7.9 49.7 %all-to-all-start = ((f32[32,4,8,256]{3,2,1,0:T(8,128)}), f32[32,4,8,256]{3,2,1,0:T(8,128)S(1)}, u32[]{:S(2)}, u32[]{:S(2)}) async-start(f32[32,4,8,256]{3,2,1,0:T(8,128)} %broadcast_in_dim.11), calls=%async_computation | async-start | bytes 2097152 | tf_op jit(solution)/shard_map/all_to_all | solution.py:263
  21.1 15.3 %collective-permute-start.2 = (f32[8,64,256]{2,1,0:T(8,128)}, f32[8,64,256]{2,1,0:T(8,128)}, u32[]{:S(2)}, u32[]{:S(2)}) collective-permute-start(f32[8,64,256]{2,1,0:T(8,128)} %get-tuple-element.34), channel_id=1, source_target_pairs={{0,1},{32,33},{64,65},{96,97}} | collective-permute-start | bytes 1572872 | tf_op jit(solution)/shard_map/ppermute | solution.py:292
  25.0 11.4 %collective-permute-start.3 = (f32[8,64,256]{2,1,0:T(8,128)}, f32[8,64,256]{2,1,0:T(8,128)}, u32[]{:S(2)}, u32[]{:S(2)}) collective-permute-start(f32[8,64,256]{2,1,0:T(8,128)} %get-tuple-element.33), channel_id=1, source_target_pairs={{0,4},{32,36},{64,68},{96,100}} | collective-permute-start | bytes 1572872 | tf_op jit(solution)/shard_map/ppermute | solution.py:292
  27.8 17.8 %collective-permute-start.4 = (f32[8,64,256]{2,1,0:T(8,128)}, f32[8,64,256]{2,1,0:T(8,128)}, u32[]{:S(2)}, u32[]{:S(2)}) collective-permute-start(f32[8,64,256]{2,1,0:T(8,128)} %get-tuple-element.30), channel_id=1, source_target_pairs={{0,8},{32,40},{64,72},{96,104}} | collective-permute-start | bytes 1572872 | tf_op jit(solution)/shard_map/ppermute | solution.py:292
  47.2 6.5 %collective-permute-start.11 = (f32[64,256]{1,0:T(8,128)S(1)}, f32[64,256]{1,0:T(8,128)S(1)}, u32[]{:S(2)}, u32[]{:S(2)}) collective-permute-start(f32[64,256]{1,0:T(8,128)S(1)} %get-tuple-element.59), channel_id=1, source_target_pairs={{0,24},{1,2},{4,5},{8,12},{32,56},{33,34},{36,37},{40,44},{64,88},... | collective-permute-start | bytes 196616 | tf_op jit(solution)/shard_map/ppermute | solution.py:302
  48.5 6.5 %collective-permute-start.10 = (f32[64,256]{1,0:T(8,128)S(1)}, f32[64,256]{1,0:T(8,128)S(1)}, u32[]{:S(2)}, u32[]{:S(2)}) collective-permute-start(f32[64,256]{1,0:T(8,128)S(1)} %get-tuple-element.60), channel_id=1, source_target_pairs={{0,3},{1,29},{4,31},{8,11},{32,35},{33,61},{36,63},{40,43},{64,67}... | collective-permute-start | bytes 196616 | tf_op jit(solution)/shard_map/ppermute | solution.py:302
  49.8 6.5 %collective-permute-start.9 = (f32[64,256]{1,0:T(8,128)S(1)}, f32[64,256]{1,0:T(8,128)S(1)}, u32[]{:S(2)}, u32[]{:S(2)}) collective-permute-start(f32[64,256]{1,0:T(8,128)S(1)} %get-tuple-element.61), channel_id=1, source_target_pairs={{0,28},{1,26},{4,20},{8,9},{32,60},{33,58},{36,52},{40,41},{64,92}... | collective-permute-start | bytes 196616 | tf_op jit(solution)/shard_map/ppermute | solution.py:302
  51.1 5.3 %collective-permute-start.8 = (f32[64,256]{1,0:T(8,128)S(1)}, f32[64,256]{1,0:T(8,128)S(1)}, u32[]{:S(2)}, u32[]{:S(2)}) collective-permute-start(f32[64,256]{1,0:T(8,128)S(1)} %get-tuple-element.62), channel_id=1, source_target_pairs={{0,27},{1,17},{4,15},{8,19},{32,59},{33,49},{36,47},{40,51},{64,91... | collective-permute-start | bytes 196616 | tf_op jit(solution)/shard_map/ppermute | solution.py:302
  52.4 4.0 %collective-permute-start.7 = (f32[64,256]{1,0:T(8,128)S(1)}, f32[64,256]{1,0:T(8,128)S(1)}, u32[]{:S(2)}, u32[]{:S(2)}) collective-permute-start(f32[64,256]{1,0:T(8,128)S(1)} %get-tuple-element.63), channel_id=1, source_target_pairs={{0,25},{1,30},{4,6},{8,13},{32,57},{33,62},{36,38},{40,45},{64,89}... | collective-permute-start | bytes 196616 | tf_op jit(solution)/shard_map/ppermute | solution.py:302
  53.7 2.7 %collective-permute-start.5 = (f32[64,256]{1,0:T(8,128)S(1)}, f32[64,256]{1,0:T(8,128)S(1)}, u32[]{:S(2)}, u32[]{:S(2)}) collective-permute-start(f32[64,256]{1,0:T(8,128)S(1)} %get-tuple-element.64), channel_id=1, source_target_pairs={{0,7},{1,22},{4,14},{8,18},{32,39},{33,54},{36,46},{40,50},{64,71}... | collective-permute-start | bytes 196616 | tf_op jit(solution)/shard_map/ppermute | solution.py:302
  55.0 2.6 %collective-permute-start.6 = (f32[64,256]{1,0:T(8,128)S(1)}, f32[64,256]{1,0:T(8,128)S(1)}, u32[]{:S(2)}, u32[]{:S(2)}) collective-permute-start(f32[64,256]{1,0:T(8,128)S(1)} %get-tuple-element.58), channel_id=1, source_target_pairs={{0,16},{1,21},{4,23},{8,10},{32,48},{33,53},{36,55},{40,42},{64,80... | collective-permute-start | bytes 196616 | tf_op jit(solution)/shard_map/ppermute | solution.py:302
  70.4 46.5 %all-to-all-start.2 = ((f32[4,8,64,256]{3,2,1,0:T(8,128)}), f32[4,8,64,256]{3,2,1,0:T(8,128)}, u32[]{:S(2)}, u32[]{:S(2)}) async-start(f32[4,8,64,256]{3,2,1,0:T(8,128)} %broadcast_in_dim.28), calls=%async_computation.2 | async-start | bytes 4194304 | tf_op jit(solution)/shard_map/all_to_all | solution.py:263
  75.0 40.4 %collective-permute-start.16 = (f32[128,1536]{1,0:T(8,128)}, f32[128,1536]{1,0:T(8,128)S(1)}, u32[]{:S(2)}, u32[]{:S(2)}) collective-permute-start(f32[128,1536]{1,0:T(8,128)} %copy-done.3), channel_id=1, source_target_pairs={{0,1},{1,0},{2,3},{3,2},{4,5},{5,4},{6,7},{7,6},{8,9},{9,8},{10,11... | collective-permute-start | bytes 2359304 | tf_op jit(solution)/shard_map/ppermute | solution.py:245
  75.0 38.9 %collective-permute-start.1 = (f32[128,1536]{1,0:T(8,128)}, f32[128,1536]{1,0:T(8,128)S(1)}, u32[]{:S(2)}, u32[]{:S(2)}) collective-permute-start(f32[128,1536]{1,0:T(8,128)} %get-tuple-element.15.own_ref), channel_id=1, source_target_pairs={{0,16},{1,17},{2,18},{3,19},{4,20},{5,21},{6,22},{7,23},{8,24},{9,... | collective-permute-start | bytes 2359304 | tf_op jit(solution)/shard_map/ppermute | solution.py:245
  79.5 60.1 %collective-permute-start.14 = (f32[1536,256]{1,0:T(8,128)}, f32[1536,256]{1,0:T(8,128)}, u32[]{:S(2)}, u32[]{:S(2)}) collective-permute-start(f32[1536,256]{1,0:T(8,128)} %dynamic-slice_bitcast_fusion), channel_id=1, source_target_pairs={{0,1},{1,0},{2,3},{3,2},{4,5},{5,4},{6,7},{7,6},{8,9},{9,8},{10,11... | collective-permute-start | bytes 4718600 | tf_op jit(solution)/shard_map/ppermute | solution.py:245
  119.4 8.2 %collective-permute-start.17 = (f32[128,768]{1,0:T(8,128)S(1)}, f32[128,768]{1,0:T(8,128)S(1)}, u32[]{:S(2)}, u32[]{:S(2)}) collective-permute-start(f32[128,768]{1,0:T(8,128)S(1)} %pad_maximum_fusion.1.own_ref), channel_id=1, source_target_pairs={{0,64},{32,96},{64,0},{96,32},{1,65},{33,97},{65,1},{97,33},{2,66}... | collective-permute-start | bytes 1179656 | tf_op jit(solution)/shard_map/ppermute | solution.py:245
  122.2 19.8 %collective-permute-start.12 = (f32[128,1536]{1,0:T(8,128)}, f32[128,1536]{1,0:T(8,128)S(1)}, u32[]{:S(2)}, u32[]{:S(2)}) collective-permute-start(f32[128,1536]{1,0:T(8,128)} %copy-done.7), channel_id=1, source_target_pairs={{0,1},{1,0},{2,3},{3,2},{4,5},{5,4},{6,7},{7,6},{8,9},{9,8},{10,11... | collective-permute-start | bytes 2359304 | tf_op jit(solution)/shard_map/ppermute | solution.py:245
  122.2 21.8 %collective-permute-start.19 = (f32[128,1536]{1,0:T(8,128)}, f32[128,1536]{1,0:T(8,128)S(1)}, u32[]{:S(2)}, u32[]{:S(2)}) collective-permute-start(f32[128,1536]{1,0:T(8,128)} %copy-done.5), channel_id=1, source_target_pairs={{0,64},{32,96},{64,0},{96,32},{1,65},{33,97},{65,1},{97,33},{2,66}... | collective-permute-start | bytes 2359304 | tf_op jit(solution)/shard_map/ppermute | solution.py:245
  128.9 23.7 %collective-permute-start.18 = (f32[128,1024]{1,0:T(8,128)S(1)}, f32[128,1024]{1,0:T(8,128)S(1)}, u32[]{:S(2)}, u32[]{:S(2)}) collective-permute-start(f32[128,1024]{1,0:T(8,128)S(1)} %pad_maximum_fusion.own_ref), channel_id=1, source_target_pairs={{0,32},{32,0},{64,96},{96,64},{1,33},{33,1},{65,97},{97,65},{2,34}... | collective-permute-start | bytes 1572872 | tf_op jit(solution)/shard_map/ppermute | solution.py:245
  139.6 14.5 %collective-permute-start.15 = (f32[1536,256]{1,0:T(8,128)}, f32[1536,256]{1,0:T(8,128)S(1)}, u32[]{:S(2)}, u32[]{:S(2)}) collective-permute-start(f32[1536,256]{1,0:T(8,128)} %collective-permute-done.14.near_ref), channel_id=1, source_target_pairs={{0,32},{32,0},{64,96},{96,64},{1,33},{33,1},{65,97},{97,65},{2,34}... | collective-permute-start | bytes 4718600 | tf_op jit(solution)/shard_map/ppermute | solution.py:245
  142.6 34.9 %collective-permute-start.13 = (f32[128,1536]{1,0:T(8,128)S(1)}, f32[128,1536]{1,0:T(8,128)S(1)}, u32[]{:S(2)}, u32[]{:S(2)}) collective-permute-start(f32[128,1536]{1,0:T(8,128)S(1)} %merge.10.own_ref), channel_id=1, source_target_pairs={{0,64},{32,96},{64,0},{96,32},{1,65},{33,97},{65,1},{97,33},{2,66}... | collective-permute-start | bytes 2359304 | tf_op jit(solution)/shard_map/ppermute | solution.py:245
  144.6 33.5 %collective-permute-start.21 = (f32[128,1536]{1,0:T(8,128)S(1)}, f32[128,1536]{1,0:T(8,128)S(1)}, u32[]{:S(2)}, u32[]{:S(2)}) collective-permute-start(f32[128,1536]{1,0:T(8,128)S(1)} %merge.14.own_ref), channel_id=1, source_target_pairs={{0,32},{32,0},{64,96},{96,64},{1,33},{33,1},{65,97},{97,65},{2,34}... | collective-permute-start | bytes 2359304 | tf_op jit(solution)/shard_map/ppermute | solution.py:245
  178.0 2.7 %collective-permute-start.20 = (f32[128,1536]{1,0:T(8,128)S(1)}, f32[128,1536]{1,0:T(8,128)S(1)}, u32[]{:S(2)}, u32[]{:S(2)}) collective-permute-start(f32[128,1536]{1,0:T(8,128)S(1)} %merge.15.own_ref), channel_id=1, source_target_pairs={{0,32},{32,0},{64,96},{96,64},{1,33},{33,1},{65,97},{97,65},{2,34}... | collective-permute-start | bytes 2359304 | tf_op jit(solution)/shard_map/ppermute | solution.py:245
  (16 other events, 238.6 us)

commit v3 on v2

--- a/solution.py
+++ b/solution.py
@@ -157,65 +157,104 @@
     )(own, received, row_map)
 
 
-def update_kernel(
-    core_ref, front_ref, panels_ref, near_ref, far_ref, lefts_ref, window_ref, inverse_ref, out_ref,
-    high_ref, low_ref, other_high_ref, other_low_ref, *, tiles,
-):
-    levels, rows, width = window_ref.shape
-    top = lefts_ref.shape[1]
+def solve(left, inverse, stacked_ref, index):
+    rows, width = left.shape
+    cols = slice(index * width, (index + 1) * width)
+    high, low = split2(product2_nt(split2(left), split2(inverse)))
+    stacked_ref[:rows, cols] = high
+    stacked_ref[rows:, cols] = low
+
+
+def stacked_product(stacked_ref, columns):
+    rows = stacked_ref.shape[0] // 2
+    high, low = split2(columns)
+    both = dot_nt(stacked_ref[...], high)
+    return both[:rows] + (both[rows:] + dot_nt(stacked_ref[:rows], low))
+
+
+def lower_kernel(front_ref, panels_ref, window_ref, inverse_ref, out_ref, stacked_ref):
+    levels = window_ref.shape[0]
+    top = out_ref.shape[0] - stacked_ref.shape[0] // 2
 
     @pl.when(pl.program_id(0) == 0)
     def _():
         for level in range(levels):
-            cols = slice(level * width, (level + 1) * width)
-            inverse = split2(inverse_ref[level])
-            left = jnp.concatenate([lefts_ref[level], window_ref[level, top:]], axis=0)
-            high_ref[:, cols], low_ref[:, cols] = split2(product2_nt(split2(left), inverse))
-            if level == 0:
-                solved = product2_nt(split2(lefts_ref[levels]), inverse)
-                other_high_ref[...], other_low_ref[...] = split2(solved)
+            solve(window_ref[level, top:], inverse_ref[level], stacked_ref, level)
 
     columns = jnp.concatenate([panels_ref[level] for level in range(levels)], axis=1)
-    update = product2_nt((high_ref[...], low_ref[...]), split2(columns))
+    out_ref[:top] = front_ref[:top]
+    out_ref[top:] = front_ref[top:] - stacked_product(stacked_ref, columns)
+
+
+def lower_rows(front, panels, window, inverse, top):
+    rows, cols = front.shape
+    levels, _, width = panels.shape
+    tile = 256
+    whole = lambda x: pl.BlockSpec(x.shape, lambda j: (0,) * x.ndim)
+    return pl.pallas_call(
+        lower_kernel,
+        grid=(cols // tile,),
+        in_specs=[
+            pl.BlockSpec((rows, tile), lambda j: (0, j)),
+            pl.BlockSpec((levels, tile, width), lambda j: (0, j, 0)),
+            whole(window),
+            whole(inverse),
+        ],
+        out_specs=pl.BlockSpec((rows, tile), lambda j: (0, j)),
+        scratch_shapes=[pltpu.VMEM((2 * (rows - top), levels * width), BF16)],
+        out_shape=jax.ShapeDtypeStruct(front.shape, F32),
+        compiler_params=pltpu.CompilerParams(vmem_limit_bytes=24 << 20),
+        cost_estimate=COST,
+        name="lower_rows",
+    )(front, panels, window, inverse)
+
+
+def upper_kernel(
+    core_ref, panels_ref, near_ref, far_ref, lefts_ref, inverse_ref, lower_ref, out_ref, stacked_ref, *, tiles,
+):
+    del lower_ref
+    levels = panels_ref.shape[0]
+
+    @pl.when(pl.program_id(0) == 0)
+    def _():
+        for index in range(levels + 1):
+            solve(lefts_ref[index], inverse_ref[index % levels], stacked_ref, index)
+
     half = pl.program_id(0) // (tiles // 2)
     other = jnp.where(half == core_ref[0], near_ref[...], far_ref[...])
-    other = product2_nt((other_high_ref[...], other_low_ref[...]), split2(other))
-    out_ref[:top] = -update[:top] - other
-    out_ref[top:] = front_ref[top:] - update[top:]
-
-
-def updated_rows(core, front, panels, near, far, lefts, window, inverse):
-    rows, cols = front.shape
-    top = lefts.shape[1]
-    levels, _, width = panels.shape
-    tile = 256
+    columns = jnp.concatenate([panels_ref[level] for level in range(levels)] + [other], axis=1)
+    out_ref[...] = -stacked_product(stacked_ref, columns)
+
+
+def upper_rows(core, panels, near, far, lefts, inverse, lower):
+    levels, cols, width = panels.shape
+    rows = lefts.shape[1]
+    tile = 512
     tiles = cols // tile
+    half = pl.BlockSpec((tile, width), lambda j, core: (lax.rem(j, tiles // 2), 0))
     whole = lambda x: pl.BlockSpec(x.shape, lambda j, core: (0,) * x.ndim)
-    half = pl.BlockSpec((tile, width), lambda j, core: (lax.rem(j, tiles // 2), 0))
-    wide = pltpu.VMEM((rows, levels * width), BF16)
-    other = pltpu.VMEM((top, width), BF16)
     return pl.pallas_call(
-        functools.partial(update_kernel, tiles=tiles),
+        functools.partial(upper_kernel, tiles=tiles),
         grid_spec=pltpu.PrefetchScalarGridSpec(
             num_scalar_prefetch=1,
             grid=(tiles,),
             in_specs=[
-                pl.BlockSpec((rows, tile), lambda j, core: (0, j)),
                 pl.BlockSpec((levels, tile, width), lambda j, core: (0, j, 0)),
                 half,
                 half,
                 whole(lefts),
-                whole(window),
                 whole(inverse),
+                pl.BlockSpec(memory_space=pl.ANY),
             ],
             out_specs=pl.BlockSpec((rows, tile), lambda j, core: (0, j)),
-            scratch_shapes=[wide, wide, other, other],
+            scratch_shapes=[pltpu.VMEM((2 * rows, (levels + 1) * width), BF16)],
         ),
-        out_shape=jax.ShapeDtypeStruct(front.shape, F32),
+        out_shape=jax.ShapeDtypeStruct(lower.shape, F32),
+        input_output_aliases={6: 0},
         compiler_params=pltpu.CompilerParams(vmem_limit_bytes=24 << 20),
         cost_estimate=COST,
-        name="updated_rows",
-    )(core, front, panels, near, far, lefts, window, inverse)
+        name="upper_rows",
+    )(core, panels, near, far, lefts, inverse, lower)
 
 
 def finish_kernel(own_ref, received_ref, map_ref, rest_ref, out_ref):
@@ -263,47 +302,27 @@
     return lax.all_to_all(copies, axis, 0, 0, tiled=True, axis_index_groups=groups)
 
 
-def dealt(parts, axis, sizes):
-    count = parts.shape[0]
-
-    def place(index):
-        found = []
-        for size in reversed(sizes):
-            found.append(index % size)
-            index //= size
-        return found
-
-    def distance(a, b):
-        steps = [(abs(i - j), size) for i, j, size in zip(place(a), place(b), reversed(sizes))]
-        return sum(min(step, size - step) for step, size in steps)
-
-    holders = [index for index in range(count) if sum(place(index)) <= 1]
-    most = -(-count // len(holders))
-    shares = {holder: [holder] for holder in holders}
-    for index in sorted(range(count), key=lambda i: (-distance(i, 0), i)):
-        if index not in holders:
-            free = [h for h in holders if len(shares[h]) < most]
-            shares[min(free, key=lambda h: (distance(h, index), len(shares[h])))].append(index)
-    for share in shares.values():
-        share += [share[0]] * (most - len(share))
-
+def dealt(parts, axis):
+    runs, each = len(parts), parts[0].shape[0]
+    first = [0, each // 2 - 1, each // 2, 1]
     device = lax.axis_index(axis)
-    held = [
-        lax.ppermute(jnp.stack([parts[i] for i in shares[holder]]), axis, [(0, holder)])
-        for holder in holders if holder
-    ]
-
-    def rest(held):
-        first = jnp.stack([parts[i] for i in shares[0]])
-        held = jnp.where(device == 0, first, functools.reduce(jnp.add, held))
-        received = [held[0]]
-        for slot in range(1, most):
-            pairs = [(h, share[slot]) for h, share in shares.items() if share[slot] != h]
-            received.append(lax.ppermute(held[slot], axis, pairs))
-        is_holder = functools.reduce(jnp.logical_or, [device == h for h in holders])
-        return jnp.where(is_holder, received[0], functools.reduce(jnp.add, received[1:]))
-
-    return held, rest
+    received = [lax.ppermute(parts[i], axis, [(0, first[i])]) for i in range(1, runs)]
+
+    def deal_on(earlier):
+        held = functools.reduce(jnp.add, after(received, earlier))
+        held = jnp.where(device == 0, parts[0], held)
+        pieces = [held[0]]
+        for slot in range(each):
+            pairs = [(first[i], i * each + slot) for i in range(runs) if first[i] != i * each + slot]
+            pieces.append(lax.ppermute(held[slot], axis, pairs))
+        return whole, pieces
+
+    def whole(pieces):
+        keeps = functools.reduce(
+            jnp.logical_or, [device == first[i] for i in range(runs) if first[i] == i * each])
+        return jnp.where(keeps, pieces[0], functools.reduce(jnp.add, pieces[1:]))
+
+    return deal_on
 
 
 def body(front, panels, diagonal_blocks, extend_maps):
@@ -315,22 +334,31 @@
     maps = [extend_maps[l, 0] for l in range(levels)]
     flips = [("fc", col_devices // 2), ("fc", 1), ("fr", row_devices // 2), ("fr", 1)]
     core = row_index % 2
+    stored = pltpu.with_memory_space_constraint(panels, pltpu.HBM)
+    stored_front = pltpu.with_memory_space_constraint(front, pltpu.HBM)
     half = cols // 2
 
     own_a, own_b = front[:top, :half], front[:top, half:]
     received_a = partner(own_a, *flips[0])
-
-    own = lax.dynamic_slice_in_dim(panels, row_index * rows, rows, 1)
-    held, rest = dealt(own.reshape(col_devices, -1, width), "fc", (4, 2, 4))
-    near = lax.dynamic_slice_in_dim(panels[0], core * half, half, 0)
-    near = partner(near, "fc", 1)
-    gathered = to_all(jnp.swapaxes(diagonal_blocks, 1, 2), "fc")
+    diagonal_part = after(jnp.swapaxes(diagonal_blocks, 1, 2), own_a)
+    gathered = to_all(diagonal_part, "fc")
+
+    first_row = after(row_index, own_a) * rows
+    own = [
+        lax.dynamic_slice(panels, (level, first_row, 0), (1, rows, width))
+        .reshape(col_devices // levels, -1, width)
+        for level in range(levels)
+    ]
+    deal_on = dealt(own, "fc")
 
     merged_a = merge(own_a, received_a, maps[0])
     received_a = partner(merged_a, *flips[1])
     received_b = partner(after(own_b, merged_a), *flips[0])
-    part = rest(after(held, merged_a))
-    part = to_all(part, "fc", [1, 2, 4])
+    whole_part, pieces = deal_on(merged_a)
+    part = to_all(whole_part(pieces), "fc", [1, 2, 4])
+
+    near = lax.dynamic_slice(panels, (0, core * half, 0), (1, half, width))[0]
+    near = partner(after(near, part), "fc", 1)
     window = to_all(part, "fc", [8, 16])
     inverse = inverses(after(gathered, part, merged_a))
     far = partner(near, "fr", 1)
@@ -344,19 +372,22 @@
     first = window[:, :top]
     turned = jnp.take(first[0], maps[1][0], axis=0, mode="clip")
     lefts = jnp.concatenate([first[0], first[1], turned], axis=1)
-    lefts = merge(lefts, partner(lefts, *flips[2]), maps[2])
+    lefts_received = partner(lefts, *flips[2])
+
+    lower = lower_rows(stored_front, stored, after(window, lefts), inverse, top)
+
+    merged_b = merge(merged_b, after(received_b, lower), maps[1])
+    merged_a = merge(merged_a, after(received_a, lower), maps[2])
+    received_b = partner(merged_b, *flips[2])
+    received_a = partner(merged_a, *flips[3])
+
+    lefts = merge(lefts, after(lefts_received, merged_a, merged_b), maps[2])
     lefts = jnp.concatenate([lefts, first[2]], axis=1)
     lefts = merge(lefts, partner(lefts, *flips[3]), maps[3])
     zero, one, other, two = [lefts[:, i * width:(i + 1) * width] for i in range(4)]
     lefts = jnp.stack([zero, one, two, first[3], other])
 
-    merged_b = merge(merged_b, received_b, maps[1])
-    merged_a = merge(merged_a, received_a, maps[2])
-    received_b = partner(merged_b, *flips[2])
-    received_a = partner(merged_a, *flips[3])
-
-    updated = updated_rows(
-        core[None], front, panels, near, far, after(lefts, merged_a, merged_b), window, inverse)
+    updated = upper_rows(core[None], stored, near, far, lefts, inverse, lower)
 
     merged_b = merge(merged_b, after(received_b, updated), maps[2])
     received_b = partner(merged_b, *flips[3])

time: 185 us -> 176 us (0.951)
  Pallas kernels: 49.2 us -> 66.8 us
  local copies, waits for them, and re-layouts: 25.9 us -> 13.2 us
  waiting for transfers between devices: 34 us -> 24.8 us
  starting transfers between devices: 60.1 us -> 56.1 us
    unnamed x43 -> x14, local copies, waits for them, and re-layouts: 13.7 us -> 1.28 us
    pallas_call x1 -> x2, Pallas kernels: 18.7 us -> 28.3 us  [the longest x1 17.3 us: lower_rows(): pl.pallas_call(lower_kernel, grid=(cols // tile,), in_specs=[pl.BlockSpec...]
    pallas_call x8, Pallas kernels: 3.97 us -> 12.1 us  [merge(): pl.pallas_call(merge_kernel, out_shape=jax.ShapeDtypeStruct(own.shape, F3...]
    ppermute x12, waiting for transfers between devices: 22.5 us -> 14.5 us  [partner(): lax.ppermute(x, axis, [(i, i ^ flip) for i in range(lax.axis_size(axis))])]
    ppermute x12, starting transfers between devices: 32.4 us -> 25.6 us  [partner(): lax.ppermute(x, axis, [(i, i ^ flip) for i in range(lax.axis_size(axis))])]
    ppermute x10 -> x11, starting transfers between devices: 17.1 us -> 22.9 us  [the longest x8 14.6 us: deal_on(): pieces.append(lax.ppermute(held[slot], axis, pairs))]
    all_to_all x2, starting transfers between devices: 10.5 us -> 7.54 us  [to_all(): lax.all_to_all(copies, axis, 0, 0, tiled=True, axis_index_groups=groups)]
    ppermute x10 -> x11, waiting for transfers between devices: 11.5 us -> 10.3 us  [the longest x3 9.67 us: dealt(): lax.ppermute(parts[i], axis, [(0, first[i])])]
  transfers between devices with their start and end apart: 24 -> 25, of which waited for: 7 -> 7; matrix products, arithmetic and copies ran while one was open for 9% -> 5% of each run, Pallas kernels for 25% -> 37%
where the time goes in v3:
time: 176 us; the launch traced here: 175 us
  Pallas kernels  66.8 us (38%)
  starting transfers between devices  56.1 us (32%)
  waiting for transfers between devices  24.8 us (14%)
  local copies, waits for them, and re-layouts  13.2 us (8%)
  blocking collectives  11.8 us (7%)
    ppermute x12, starting transfers between devices, partner(): lax.ppermute(x, axis, [(i, i ^ flip) for i in range(lax.axis_size(axis))])  25.6 us
    pallas_call x1, Pallas kernels, inverses(): pl.pallas_call(functools.partial(inverse_kernel, width=width), out_shape=...  21.4 us
    pallas_call x1, Pallas kernels, lower_rows(): pl.pallas_call(lower_kernel, grid=(cols // tile,), in_specs=[pl.BlockSpec...  17.3 us
    ppermute x8, starting transfers between devices, deal_on(): pieces.append(lax.ppermute(held[slot], axis, pairs))  14.6 us
    ppermute x12, waiting for transfers between devices, partner(): lax.ppermute(x, axis, [(i, i ^ flip) for i in range(lax.axis_size(axis))])  14.5 us
    pallas_call x8, Pallas kernels, merge(): pl.pallas_call(merge_kernel, out_shape=jax.ShapeDtypeStruct(own.shape, F3...  12.1 us
    all_to_all x1, blocking collectives, to_all(): lax.all_to_all(copies, axis, 0, 0, tiled=True, axis_index_groups=groups)  11.8 us
    pallas_call x1, Pallas kernels, upper_rows(): pl.pallas_call(functools.partial(upper_kernel, tiles=tiles), grid_spec=pl...  11 us
  transfers between devices with their start and end apart: 25, of which 7 were waited for; matrix products, arithmetic and copies ran while one was open for 5% of the time, Pallas kernels for 37%

profile of v3, /device:TPU:1, one launch (start us, length us, event | category | flops | bytes accessed | tf_op | source)
XLA Modules:
  0.0 174.7 jit_solution(13568344908735260947)
XLA Ops:
  0.0 2.4 %fusion.4 = (f32[128,1536]{1,0:T(8,128)S(1)}, f32[128,1536]{1,0:T(8,128)}) fusion(f32[512,3072]{1,0:T(8,128)} %front_ref.1), kind=kLoop, calls=%fused_computation.36 | loop fusion | bytes 3145728 | tf_op jit(solution)/shard_map/slice | solution.py:341
  2.4 4.4 %collective-permute-start = (f32[128,1536]{1,0:T(8,128)S(1)}, f32[128,1536]{1,0:T(8,128)S(1)}, u32[]{:S(2)}, u32[]{:S(2)}) collective-permute-start(f32[128,1536]{1,0:T(8,128)S(1)} %get-tuple-element.41.own_ref), channel_id=1, source_target_pairs={{0,16},{1,17},{2,18},{3,19},{4,20},{5,21},{6,22},{7,23},{8,24},{9,... | collective-permute-start | bytes 2359304 | tf_op jit(solution)/shard_map/ppermute | solution.py:284
  6.8 2.7 %constant_dynamic-slice_fusion = (f32[1,512,256]{2,1,0:T(8,128)}, f32[1,512,256]{2,1,0:T(8,128)}, f32[1,512,256]{2,1,0:T(8,128)}, f32[1,512,256]{2,1,0:T(8,128)S(1)}) fusion(f32[4,3072,256]{2,1,0:T(8,128)} %panels_ref.3, s32[]{:T(128)S(6)} %select_n.34), kind=kLoop, calls=%fused_computation.27 | loop fusion | bytes 4194308 | tf_op jit(solution)/shard_map/dynamic_slice | solution.py:348
  9.5 3.9 %collective-permute-start.3 = (f32[8,64,256]{2,1,0:T(8,128)}, f32[8,64,256]{2,1,0:T(8,128)}, u32[]{:S(2)}, u32[]{:S(2)}) collective-permute-start(f32[8,64,256]{2,1,0:T(8,128)} %bitcast.4), channel_id=1, source_target_pairs={{0,4},{32,36},{64,68},{96,100}} | collective-permute-start | bytes 1572872 | tf_op jit(solution)/shard_map/ppermute | solution.py:309
  15.5 2.4 %collective-permute-start.2 = (f32[8,64,256]{2,1,0:T(8,128)}, f32[8,64,256]{2,1,0:T(8,128)}, u32[]{:S(2)}, u32[]{:S(2)}) collective-permute-start(f32[8,64,256]{2,1,0:T(8,128)} %bitcast.3), channel_id=1, source_target_pairs={{0,3},{32,35},{64,67},{96,99}} | collective-permute-start | bytes 1572872 | tf_op jit(solution)/shard_map/ppermute | solution.py:309
  18.9 3.9 %all-to-all-start = ((f32[32,4,8,256]{3,2,1,0:T(8,128)}), f32[32,4,8,256]{3,2,1,0:T(8,128)S(1)}, u32[]{:S(2)}, u32[]{:S(2)}) async-start(f32[32,4,8,256]{3,2,1,0:T(8,128)} %broadcast_in_dim.11), calls=%async_computation | async-start | bytes 2097152 | tf_op jit(solution)/shard_map/all_to_all | solution.py:302
  27.3 7.8 %collective-permute-done.2 = f32[8,64,256]{2,1,0:T(8,128)} collective-permute-done((f32[8,64,256]{2,1,0:T(8,128)}, f32[8,64,256]{2,1,0:T(8,128)}, u32[]{:S(2)}, u32[]{:S(2)}) %collective-permute-start.2) | collective-permute-done | bytes 524320 | tf_op jit(solution)/shard_map/ppermute | solution.py:309
  43.2 6.2 %collective-permute-start.8 = (f32[64,256]{1,0:T(8,128)S(1)}, f32[64,256]{1,0:T(8,128)S(1)}, u32[]{:S(2)}, u32[]{:S(2)}) collective-permute-start(f32[64,256]{1,0:T(8,128)S(1)} %get-tuple-element.51), channel_id=1, source_target_pairs={{0,3},{3,11},{4,19},{1,27},{32,35},{35,43},{36,51},{33,59},{64,67}... | collective-permute-start | bytes 196616 | tf_op jit(solution)/shard_map/ppermute | solution.py:317
  52.1 11.8 %all_to_all.15 = f32[8,64,256]{2,1,0:T(8,128)S(1)} all-to-all(f32[8,64,256]{2,1,0:T(8,128)S(1)} %broadcast_in_dim.12), channel_id=1, replica_groups={{0,1,2,3,4,5,6,7},{8,9,10,11,12,13,14,15},{16,17,18,19,20,21,22,23},{24..., dimensions={0} | all-to-all | bytes 1048576 | tf_op jit(solution)/shard_map/all_to_all | solution.py:302
  65.5 3.6 %all-to-all-start.2 = ((f32[4,8,64,256]{3,2,1,0:T(8,128)}), f32[4,8,64,256]{3,2,1,0:T(8,128)S(1)}, u32[]{:S(2)}, u32[]{:S(2)}) async-start(f32[4,8,64,256]{3,2,1,0:T(8,128)} %broadcast_in_dim.14), calls=%async_computation.2 | async-start | bytes 4194304 | tf_op jit(solution)/shard_map/all_to_all | solution.py:302
  69.2 2.9 %collective-permute-start.1 = (f32[128,1536]{1,0:T(8,128)}, f32[128,1536]{1,0:T(8,128)}, u32[]{:S(2)}, u32[]{:S(2)}) collective-permute-start(f32[128,1536]{1,0:T(8,128)} %get-tuple-element.21.own_ref), channel_id=1, source_target_pairs={{0,16},{1,17},{2,18},{3,19},{4,20},{5,21},{6,22},{7,23},{8,24},{9,... | collective-permute-start | bytes 2359304 | tf_op jit(solution)/shard_map/ppermute | solution.py:284
  72.1 2.7 %dynamic-slice_bitcast_fusion = f32[1536,256]{1,0:T(8,128)} fusion(f32[4,3072,256]{2,1,0:T(8,128)} %panels_ref.3, s32[]{:T(128)S(6)} %select_n.38), kind=kLoop, calls=%fused_computation.1 | loop fusion | bytes 3145732 | tf_op jit(solution)/shard_map/squeeze | solution.py:360
  77.4 21.4 %symmetric_inverses.1.inverse_ref = f32[4,256,256]{2,1,0:T(8,128)S(1)} custom-call(f32[32,4,8,256]{3,2,1,0:T(8,128)S(1)} %copy-done.1), custom_call_target="tpu_custom_call" | custom-call | flops 1 | bytes 1 | tf_op jit(solution)/shard_map/symmetric_inverses/pallas_call | solution.py:112
  98.8 6.4 %collective-permute-done.1.received_ref = f32[128,1536]{1,0:T(8,128)} collective-permute-done((f32[128,1536]{1,0:T(8,128)}, f32[128,1536]{1,0:T(8,128)}, u32[]{:S(2)}, u32[]{:S(2)}) %collective-permute-start.1) | collective-permute-done | bytes 786464 | tf_op jit(solution)/shard_map/ppermute | solution.py:284
  105.2 2.8 %merge.9.own_ref = f32[128,1536]{1,0:T(8,128)} custom-call(f32[128,1536]{1,0:T(8,128)} %get-tuple-element.21.own_ref, f32[128,1536]{1,0:T(8,128)} %collective-permute-done.1.received_ref, s32[1,128]{1,0:T(1,128)S(1)} %get-tuple-element.57.map_ref), custom_call_target="tpu_custom_call" | custom-call | flops 1 | bytes 1 | tf_op jit(solution)/shard_map/merge/pallas_call | solution.py:149
  108.0 2.8 %merge.10.own_ref = f32[128,1536]{1,0:T(8,128)} custom-call(f32[128,1536]{1,0:T(8,128)} %merge.8.own_ref, f32[128,1536]{1,0:T(8,128)} %collective-permute-done.14.received_ref, s32[1,128]{1,0:T(1,128)S(1)} %get-tuple-element.56.map_ref), custom_call_target="tpu_custom_call" | custom-call | flops 1 | bytes 1 | tf_op jit(solution)/shard_map/merge/pallas_call | solution.py:149
  110.8 3.2 %collective-permute-start.19 = (f32[128,1536]{1,0:T(8,128)}, f32[128,1536]{1,0:T(8,128)}, u32[]{:S(2)}, u32[]{:S(2)}) collective-permute-start(f32[128,1536]{1,0:T(8,128)} %merge.10.own_ref), channel_id=1, source_target_pairs={{0,64},{32,96},{64,0},{96,32},{1,65},{33,97},{65,1},{97,33},{2,66}... | collective-permute-start | bytes 2359304 | tf_op jit(solution)/shard_map/ppermute | solution.py:284
  115.6 17.3 %lower_rows.1.lower_ref = f32[512,3072]{1,0:T(8,128)} custom-call(f32[512,3072]{1,0:T(8,128)} %front_ref.1, f32[4,3072,256]{2,1,0:T(8,128)} %panels_ref.3, f32[4,512,256]{2,1,0:T(8,128)S(1)} %bitcast.60, f32[4,256,256]{2,1,0:T(8,128)S(1)} %symmetric_inverses.1.inverse_ref), custom_call_target="tpu_custom_call" | custom-call | flops 1 | bytes 1 | tf_op jit(solution)/shard_map/lower_rows/pallas_call | solution.py:194
  138.5 8.8 %collective-permute-start.20 = (f32[128,1024]{1,0:T(8,128)S(1)}, f32[128,1024]{1,0:T(8,128)S(1)}, u32[]{:S(2)}, u32[]{:S(2)}) collective-permute-start(f32[128,1024]{1,0:T(8,128)S(1)} %pad_maximum_fusion.own_ref), channel_id=1, source_target_pairs={{0,32},{32,0},{64,96},{96,64},{1,33},{33,1},{65,97},{97,65},{2,34}... | collective-permute-start | bytes 1572872 | tf_op jit(solution)/shard_map/ppermute | solution.py:284
  147.6 2.8 %collective-permute-start.15 = (f32[128,1536]{1,0:T(8,128)S(1)}, f32[128,1536]{1,0:T(8,128)S(1)}, u32[]{:S(2)}, u32[]{:S(2)}) collective-permute-start(f32[128,1536]{1,0:T(8,128)S(1)} %merge.11.own_ref), channel_id=1, source_target_pairs={{0,64},{32,96},{64,0},{96,32},{1,65},{33,97},{65,1},{97,33},{2,66}... | collective-permute-start | bytes 2359304 | tf_op jit(solution)/shard_map/ppermute | solution.py:284
  151.4 11.0 %upper_rows.1.rest_ref = f32[512,3072]{1,0:T(8,128)} custom-call(s32[1]{0:T(128)} %bitcast.19.core_ref, f32[4,3072,256]{2,1,0:T(8,128)} %panels_ref.3, f32[1536,256]{1,0:T(8,128)} %collective-permute-done.16.near_ref, f32[1536,256]{1,0:T(8,128)S(1)} %collective-permute-done.17.far_ref, ...), custom_call_target="tpu_custom_call", output_to_operand_aliasing={{}: (6, {})} | custom-call | flops 1 | bytes 1 | tf_op jit(solution)/shard_map/upper_rows/pallas_call | solution.py:236
  162.3 5.6 %collective-permute-done.15.received_ref = f32[128,1536]{1,0:T(8,128)S(1)} collective-permute-done((f32[128,1536]{1,0:T(8,128)S(1)}, f32[128,1536]{1,0:T(8,128)S(1)}, u32[]{:S(2)}, u32[]{:S(2)}) %collective-permute-start.15) | collective-permute-done | bytes 786464 | tf_op jit(solution)/shard_map/ppermute | solution.py:284
  169.6 2.5 %finished.2.rest_ref = f32[512,3072]{1,0:T(8,128)} custom-call(f32[128,1536]{1,0:T(8,128)S(1)} %merge.12.own_ref, f32[128,1536]{1,0:T(8,128)S(1)} %collective-permute-done.22.received_ref, s32[1,128]{1,0:T(1,128)S(1)} %get-tuple-element.54.map_ref, f32[512,3072]{1,0:T(8,128)} %upper_rows.1.rest_ref), custom_call_target="tpu_custom_call", output_to_operand_aliasing={{}: (3, {})} | custom-call | flops 1 | bytes 1 | tf_op jit(solution)/shard_map/finished/pallas_call | solution.py:270
  172.2 2.6 %finished.3 = f32[512,3072]{1,0:T(8,128)} custom-call(f32[128,1536]{1,0:T(8,128)S(1)} %merge.15.own_ref, f32[128,1536]{1,0:T(8,128)S(1)} %collective-permute-done.21.received_ref, s32[1,128]{1,0:T(1,128)S(1)} %get-tuple-element.54.map_ref, f32[512,3072]{1,0:T(8,128)} %finished.2.rest_ref), custom_call_target="tpu_custom_call", output_to_operand_aliasing={{}: (3, {})} | custom-call | flops 1 | bytes 1 | tf_op jit(solution)/shard_map/finished/pallas_call | solution.py:270
  (70 shorter events, 32.5 us)
Async XLA Ops:
  2.4 21.7 %collective-permute-start = (f32[128,1536]{1,0:T(8,128)S(1)}, f32[128,1536]{1,0:T(8,128)S(1)}, u32[]{:S(2)}, u32[]{:S(2)}) collective-permute-start(f32[128,1536]{1,0:T(8,128)S(1)} %get-tuple-element.41.own_ref), channel_id=1, source_target_pairs={{0,16},{1,17},{2,18},{3,19},{4,20},{5,21},{6,22},{7,23},{8,24},{9,... | collective-permute-start | bytes 2359304 | tf_op jit(solution)/shard_map/ppermute | solution.py:284
  9.5 16.0 %collective-permute-start.3 = (f32[8,64,256]{2,1,0:T(8,128)}, f32[8,64,256]{2,1,0:T(8,128)}, u32[]{:S(2)}, u32[]{:S(2)}) collective-permute-start(f32[8,64,256]{2,1,0:T(8,128)} %bitcast.4), channel_id=1, source_target_pairs={{0,4},{32,36},{64,68},{96,100}} | collective-permute-start | bytes 1572872 | tf_op jit(solution)/shard_map/ppermute | solution.py:309
  13.4 13.9 %collective-permute-start.4 = (f32[8,64,256]{2,1,0:T(8,128)}, f32[8,64,256]{2,1,0:T(8,128)}, u32[]{:S(2)}, u32[]{:S(2)}) collective-permute-start(f32[8,64,256]{2,1,0:T(8,128)} %bitcast.5), channel_id=1, source_target_pairs={{0,1},{32,33},{64,65},{96,97}} | collective-permute-start | bytes 1572872 | tf_op jit(solution)/shard_map/ppermute | solution.py:309
  15.5 19.7 %collective-permute-start.2 = (f32[8,64,256]{2,1,0:T(8,128)}, f32[8,64,256]{2,1,0:T(8,128)}, u32[]{:S(2)}, u32[]{:S(2)}) collective-permute-start(f32[8,64,256]{2,1,0:T(8,128)} %bitcast.3), channel_id=1, source_target_pairs={{0,3},{32,35},{64,67},{96,99}} | collective-permute-start | bytes 1572872 | tf_op jit(solution)/shard_map/ppermute | solution.py:309
  18.9 33.1 %all-to-all-start = ((f32[32,4,8,256]{3,2,1,0:T(8,128)}), f32[32,4,8,256]{3,2,1,0:T(8,128)S(1)}, u32[]{:S(2)}, u32[]{:S(2)}) async-start(f32[32,4,8,256]{3,2,1,0:T(8,128)} %broadcast_in_dim.11), calls=%async_computation | async-start | bytes 2097152 | tf_op jit(solution)/shard_map/all_to_all | solution.py:302
  36.7 6.5 %collective-permute-start.6 = (f32[64,256]{1,0:T(8,128)S(1)}, f32[64,256]{1,0:T(8,128)S(1)}, u32[]{:S(2)}, u32[]{:S(2)}) collective-permute-start(f32[64,256]{1,0:T(8,128)S(1)} %get-tuple-element.46), channel_id=1, source_target_pairs={{0,1},{3,9},{4,17},{1,25},{32,33},{35,41},{36,49},{33,57},{64,65},... | collective-permute-start | bytes 196616 | tf_op jit(solution)/shard_map/ppermute | solution.py:317
  38.0 11.4 %collective-permute-start.12 = (f32[64,256]{1,0:T(8,128)S(1)}, f32[64,256]{1,0:T(8,128)S(1)}, u32[]{:S(2)}, u32[]{:S(2)}) collective-permute-start(f32[64,256]{1,0:T(8,128)S(1)} %get-tuple-element.47), channel_id=1, source_target_pairs={{0,7},{3,15},{4,23},{1,31},{32,39},{35,47},{36,55},{33,63},{64,71}... | collective-permute-start | bytes 196616 | tf_op jit(solution)/shard_map/ppermute | solution.py:317
  39.3 11.4 %collective-permute-start.11 = (f32[64,256]{1,0:T(8,128)S(1)}, f32[64,256]{1,0:T(8,128)S(1)}, u32[]{:S(2)}, u32[]{:S(2)}) collective-permute-start(f32[64,256]{1,0:T(8,128)S(1)} %get-tuple-element.48), channel_id=1, source_target_pairs={{0,6},{3,14},{4,22},{1,30},{32,38},{35,46},{36,54},{33,62},{64,70}... | collective-permute-start | bytes 196616 | tf_op jit(solution)/shard_map/ppermute | solution.py:317
  40.6 10.8 %collective-permute-start.10 = (f32[64,256]{1,0:T(8,128)S(1)}, f32[64,256]{1,0:T(8,128)S(1)}, u32[]{:S(2)}, u32[]{:S(2)}) collective-permute-start(f32[64,256]{1,0:T(8,128)S(1)} %get-tuple-element.49), channel_id=1, source_target_pairs={{0,5},{3,13},{4,21},{1,29},{32,37},{35,45},{36,53},{33,61},{64,69}... | collective-permute-start | bytes 196616 | tf_op jit(solution)/shard_map/ppermute | solution.py:317
  41.9 9.5 %collective-permute-start.9 = (f32[64,256]{1,0:T(8,128)S(1)}, f32[64,256]{1,0:T(8,128)S(1)}, u32[]{:S(2)}, u32[]{:S(2)}) collective-permute-start(f32[64,256]{1,0:T(8,128)S(1)} %get-tuple-element.50), channel_id=1, source_target_pairs={{0,4},{3,12},{4,20},{1,28},{32,36},{35,44},{36,52},{33,60},{64,68}... | collective-permute-start | bytes 196616 | tf_op jit(solution)/shard_map/ppermute | solution.py:317
  43.2 8.2 %collective-permute-start.8 = (f32[64,256]{1,0:T(8,128)S(1)}, f32[64,256]{1,0:T(8,128)S(1)}, u32[]{:S(2)}, u32[]{:S(2)}) collective-permute-start(f32[64,256]{1,0:T(8,128)S(1)} %get-tuple-element.51), channel_id=1, source_target_pairs={{0,3},{3,11},{4,19},{1,27},{32,35},{35,43},{36,51},{33,59},{64,67}... | collective-permute-start | bytes 196616 | tf_op jit(solution)/shard_map/ppermute | solution.py:317
  49.4 2.6 %collective-permute-start.7 = (f32[64,256]{1,0:T(8,128)S(1)}, f32[64,256]{1,0:T(8,128)S(1)}, u32[]{:S(2)}, u32[]{:S(2)}) collective-permute-start(f32[64,256]{1,0:T(8,128)S(1)} %get-tuple-element.52), channel_id=1, source_target_pairs={{0,2},{3,10},{4,18},{1,26},{32,34},{35,42},{36,50},{33,58},{64,66}... | collective-permute-start | bytes 196616 | tf_op jit(solution)/shard_map/ppermute | solution.py:317
  65.5 48.5 %all-to-all-start.2 = ((f32[4,8,64,256]{3,2,1,0:T(8,128)}), f32[4,8,64,256]{3,2,1,0:T(8,128)S(1)}, u32[]{:S(2)}, u32[]{:S(2)}) async-start(f32[4,8,64,256]{3,2,1,0:T(8,128)} %broadcast_in_dim.14), calls=%async_computation.2 | async-start | bytes 4194304 | tf_op jit(solution)/shard_map/all_to_all | solution.py:302
  69.2 36.0 %collective-permute-start.1 = (f32[128,1536]{1,0:T(8,128)}, f32[128,1536]{1,0:T(8,128)}, u32[]{:S(2)}, u32[]{:S(2)}) collective-permute-start(f32[128,1536]{1,0:T(8,128)} %get-tuple-element.21.own_ref), channel_id=1, source_target_pairs={{0,16},{1,17},{2,18},{3,19},{4,20},{5,21},{6,22},{7,23},{8,24},{9,... | collective-permute-start | bytes 2359304 | tf_op jit(solution)/shard_map/ppermute | solution.py:284
  72.1 35.9 %collective-permute-start.14 = (f32[128,1536]{1,0:T(8,128)}, f32[128,1536]{1,0:T(8,128)}, u32[]{:S(2)}, u32[]{:S(2)}) collective-permute-start(f32[128,1536]{1,0:T(8,128)} %merge.8.own_ref), channel_id=1, source_target_pairs={{0,1},{1,0},{2,3},{3,2},{4,5},{5,4},{6,7},{7,6},{8,9},{9,8},{10,11... | collective-permute-start | bytes 2359304 | tf_op jit(solution)/shard_map/ppermute | solution.py:284
  74.8 72.5 %collective-permute-start.16 = (f32[1536,256]{1,0:T(8,128)}, f32[1536,256]{1,0:T(8,128)}, u32[]{:S(2)}, u32[]{:S(2)}) collective-permute-start(f32[1536,256]{1,0:T(8,128)} %dynamic-slice_bitcast_fusion), channel_id=1, source_target_pairs={{0,1},{1,0},{2,3},{3,2},{4,5},{5,4},{6,7},{7,6},{8,9},{9,8},{10,11... | collective-permute-start | bytes 4718600 | tf_op jit(solution)/shard_map/ppermute | solution.py:284
  108.0 26.2 %collective-permute-start.13 = (f32[128,1536]{1,0:T(8,128)}, f32[128,1536]{1,0:T(8,128)}, u32[]{:S(2)}, u32[]{:S(2)}) collective-permute-start(f32[128,1536]{1,0:T(8,128)} %merge.9.own_ref), channel_id=1, source_target_pairs={{0,1},{1,0},{2,3},{3,2},{4,5},{5,4},{6,7},{7,6},{8,9},{9,8},{10,11... | collective-permute-start | bytes 2359304 | tf_op jit(solution)/shard_map/ppermute | solution.py:284
  110.8 25.3 %collective-permute-start.19 = (f32[128,1536]{1,0:T(8,128)}, f32[128,1536]{1,0:T(8,128)}, u32[]{:S(2)}, u32[]{:S(2)}) collective-permute-start(f32[128,1536]{1,0:T(8,128)} %merge.10.own_ref), channel_id=1, source_target_pairs={{0,64},{32,96},{64,0},{96,32},{1,65},{33,97},{65,1},{97,33},{2,66}... | collective-permute-start | bytes 2359304 | tf_op jit(solution)/shard_map/ppermute | solution.py:284
  115.5 22.5 %collective-permute-start.18 = (f32[128,768]{1,0:T(8,128)S(1)}, f32[128,768]{1,0:T(8,128)S(1)}, u32[]{:S(2)}, u32[]{:S(2)}) collective-permute-start(f32[128,768]{1,0:T(8,128)S(1)} %pad_maximum_fusion.1.own_ref), channel_id=1, source_target_pairs={{0,64},{32,96},{64,0},{96,32},{1,65},{33,97},{65,1},{97,33},{2,66}... | collective-permute-start | bytes 1179656 | tf_op jit(solution)/shard_map/ppermute | solution.py:284
  138.5 12.4 %collective-permute-start.20 = (f32[128,1024]{1,0:T(8,128)S(1)}, f32[128,1024]{1,0:T(8,128)S(1)}, u32[]{:S(2)}, u32[]{:S(2)}) collective-permute-start(f32[128,1024]{1,0:T(8,128)S(1)} %pad_maximum_fusion.own_ref), channel_id=1, source_target_pairs={{0,32},{32,0},{64,96},{96,64},{1,33},{33,1},{65,97},{97,65},{2,34}... | collective-permute-start | bytes 1572872 | tf_op jit(solution)/shard_map/ppermute | solution.py:284
  147.3 4.1 %collective-permute-start.17 = (f32[1536,256]{1,0:T(8,128)}, f32[1536,256]{1,0:T(8,128)S(1)}, u32[]{:S(2)}, u32[]{:S(2)}) collective-permute-start(f32[1536,256]{1,0:T(8,128)} %collective-permute-done.16.near_ref), channel_id=1, source_target_pairs={{0,32},{32,0},{64,96},{96,64},{1,33},{33,1},{65,97},{97,65},{2,34}... | collective-permute-start | bytes 4718600 | tf_op jit(solution)/shard_map/ppermute | solution.py:284
  147.6 20.4 %collective-permute-start.15 = (f32[128,1536]{1,0:T(8,128)S(1)}, f32[128,1536]{1,0:T(8,128)S(1)}, u32[]{:S(2)}, u32[]{:S(2)}) collective-permute-start(f32[128,1536]{1,0:T(8,128)S(1)} %merge.11.own_ref), channel_id=1, source_target_pairs={{0,64},{32,96},{64,0},{96,32},{1,65},{33,97},{65,1},{97,33},{2,66}... | collective-permute-start | bytes 2359304 | tf_op jit(solution)/shard_map/ppermute | solution.py:284
  150.3 19.3 %collective-permute-start.22 = (f32[128,1536]{1,0:T(8,128)S(1)}, f32[128,1536]{1,0:T(8,128)S(1)}, u32[]{:S(2)}, u32[]{:S(2)}) collective-permute-start(f32[128,1536]{1,0:T(8,128)S(1)} %merge.12.own_ref), channel_id=1, source_target_pairs={{0,32},{32,0},{64,96},{96,64},{1,33},{33,1},{65,97},{97,65},{2,34}... | collective-permute-start | bytes 2359304 | tf_op jit(solution)/shard_map/ppermute | solution.py:284
  168.5 3.7 %collective-permute-start.21 = (f32[128,1536]{1,0:T(8,128)S(1)}, f32[128,1536]{1,0:T(8,128)S(1)}, u32[]{:S(2)}, u32[]{:S(2)}) collective-permute-start(f32[128,1536]{1,0:T(8,128)S(1)} %merge.15.own_ref), channel_id=1, source_target_pairs={{0,32},{32,0},{64,96},{96,64},{1,33},{33,1},{65,97},{97,65},{2,34}... | collective-permute-start | bytes 2359304 | tf_op jit(solution)/shard_map/ppermute | solution.py:284
  (6 other events, 79.6 us)

commit v4 on v3

--- a/solution.py
+++ b/solution.py
@@ -172,7 +172,8 @@
     return both[:rows] + (both[rows:] + dot_nt(stacked_ref[:rows], low))
 
 
-def lower_kernel(front_ref, panels_ref, window_ref, inverse_ref, out_ref, stacked_ref):
+def lower_kernel(front_ref, panels_ref, window_ref, inverse_ref, *rest):
+    out_ref, stacked_ref = rest[-2:]
     levels = window_ref.shape[0]
     top = out_ref.shape[0] - stacked_ref.shape[0] // 2
 
@@ -186,27 +187,31 @@
     out_ref[top:] = front_ref[top:] - stacked_product(stacked_ref, columns)
 
 
-def lower_rows(front, panels, window, inverse, top):
+def lower_rows(front, panels, window, inverse, top, part, into=None):
     rows, cols = front.shape
     levels, _, width = panels.shape
     tile = 256
+    tiles = cols // tile // 2
+    skip = part * tiles
+    extra = [] if into is None else [into]
     whole = lambda x: pl.BlockSpec(x.shape, lambda j: (0,) * x.ndim)
     return pl.pallas_call(
         lower_kernel,
-        grid=(cols // tile,),
+        grid=(tiles,),
         in_specs=[
-            pl.BlockSpec((rows, tile), lambda j: (0, j)),
-            pl.BlockSpec((levels, tile, width), lambda j: (0, j, 0)),
+            pl.BlockSpec((rows, tile), lambda j: (0, skip + j)),
+            pl.BlockSpec((levels, tile, width), lambda j: (0, skip + j, 0)),
             whole(window),
             whole(inverse),
-        ],
-        out_specs=pl.BlockSpec((rows, tile), lambda j: (0, j)),
+        ] + [pl.BlockSpec(memory_space=pl.ANY)] * len(extra),
+        out_specs=pl.BlockSpec((rows, tile), lambda j: (0, skip + j)),
         scratch_shapes=[pltpu.VMEM((2 * (rows - top), levels * width), BF16)],
         out_shape=jax.ShapeDtypeStruct(front.shape, F32),
+        input_output_aliases={4: 0} if extra else {},
         compiler_params=pltpu.CompilerParams(vmem_limit_bytes=24 << 20),
         cost_estimate=COST,
         name="lower_rows",
-    )(front, panels, window, inverse)
+    )(front, panels, window, inverse, *extra)
 
 
 def upper_kernel(
@@ -374,14 +379,17 @@
     lefts = jnp.concatenate([first[0], first[1], turned], axis=1)
     lefts_received = partner(lefts, *flips[2])
 
-    lower = lower_rows(stored_front, stored, after(window, lefts), inverse, top)
+    lower = lower_rows(stored_front, stored, after(window, lefts), inverse, top, 0)
 
     merged_b = merge(merged_b, after(received_b, lower), maps[1])
     merged_a = merge(merged_a, after(received_a, lower), maps[2])
     received_b = partner(merged_b, *flips[2])
     received_a = partner(merged_a, *flips[3])
 
-    lefts = merge(lefts, after(lefts_received, merged_a, merged_b), maps[2])
+    lower = lower_rows(
+        stored_front, stored, after(window, merged_a, merged_b), inverse, top, 1, lower)
+
+    lefts = merge(lefts, after(lefts_received, lower), maps[2])
     lefts = jnp.concatenate([lefts, first[2]], axis=1)
     lefts = merge(lefts, partner(lefts, *flips[3]), maps[3])
     zero, one, other, two = [lefts[:, i * width:(i + 1) * width] for i in range(4)]

time: 176 us -> 181 us (1.028)
  waiting for transfers between devices: 24.8 us -> 27.4 us
  Pallas kernels: 66.8 us -> 69.1 us
    ppermute x12, waiting for transfers between devices: 14.5 us -> 19.5 us  [partner(): lax.ppermute(x, axis, [(i, i ^ flip) for i in range(lax.axis_size(axis))])]
    ppermute x3, waiting for transfers between devices: 9.67 us -> 6.64 us  [dealt(): lax.ppermute(parts[i], axis, [(0, first[i])])]
    pallas_call x1 -> x2, Pallas kernels: 17.3 us -> 19.6 us  [lower_rows(): pl.pallas_call(lower_kernel, grid=(tiles,), in_specs=[pl.BlockSpec((rows,...]
where the time goes in v4:
time: 181 us; the launch traced here: 180 us
  Pallas kernels  69.1 us (38%)
  starting transfers between devices  57.3 us (32%)
  waiting for transfers between devices  27.4 us (15%)
  local copies, waits for them, and re-layouts  13.2 us (7%)
  blocking collectives  10.7 us (6%)
    ppermute x12, starting transfers between devices, partner(): lax.ppermute(x, axis, [(i, i ^ flip) for i in range(lax.axis_size(axis))])  26.9 us
    pallas_call x1, Pallas kernels, inverses(): pl.pallas_call(functools.partial(inverse_kernel, width=width), out_shape=...  21.4 us
    pallas_call x2, Pallas kernels, lower_rows(): pl.pallas_call(lower_kernel, grid=(tiles,), in_specs=[pl.BlockSpec((rows,...  19.6 us
    ppermute x12, waiting for transfers between devices, partner(): lax.ppermute(x, axis, [(i, i ^ flip) for i in range(lax.axis_size(axis))])  19.5 us
    ppermute x8, starting transfers between devices, deal_on(): pieces.append(lax.ppermute(held[slot], axis, pairs))  13.3 us
    pallas_call x8, Pallas kernels, merge(): pl.pallas_call(merge_kernel, out_shape=jax.ShapeDtypeStruct(own.shape, F3...  12.1 us
    pallas_call x1, Pallas kernels, upper_rows(): pl.pallas_call(functools.partial(upper_kernel, tiles=tiles), grid_spec=pl...  11 us
    all_to_all x1, blocking collectives, to_all(): lax.all_to_all(copies, axis, 0, 0, tiled=True, axis_index_groups=groups)  10.7 us
  transfers between devices with their start and end apart: 25, of which 7 were waited for; matrix products, arithmetic and copies ran while one was open for 5% of the time, Pallas kernels for 37%

profile of v4, /device:TPU:1, one launch (start us, length us, event | category | flops | bytes accessed | tf_op | source)
XLA Modules:
  0.0 179.7 jit_solution(18143863956467797942)
XLA Ops:
  2.4 4.4 %collective-permute-start = (f32[128,1536]{1,0:T(8,128)S(1)}, f32[128,1536]{1,0:T(8,128)S(1)}, u32[]{:S(2)}, u32[]{:S(2)}) collective-permute-start(f32[128,1536]{1,0:T(8,128)S(1)} %get-tuple-element.43.own_ref), channel_id=1, source_target_pairs={{0,16},{1,17},{2,18},{3,19},{4,20},{5,21},{6,22},{7,23},{8,24},{9,... | collective-permute-start | bytes 2359304 | tf_op jit(solution)/shard_map/ppermute | solution.py:289
  6.8 2.7 %constant_dynamic-slice_fusion = (f32[1,512,256]{2,1,0:T(8,128)}, f32[1,512,256]{2,1,0:T(8,128)}, f32[1,512,256]{2,1,0:T(8,128)}, f32[1,512,256]{2,1,0:T(8,128)S(1)}) fusion(f32[4,3072,256]{2,1,0:T(8,128)} %panels_ref.5, s32[]{:T(128)S(6)} %select_n.34), kind=kLoop, calls=%fused_computation.27 | loop fusion | bytes 4194308 | tf_op jit(solution)/shard_map/dynamic_slice | solution.py:353
  9.5 5.4 %collective-permute-start.2 = (f32[8,64,256]{2,1,0:T(8,128)}, f32[8,64,256]{2,1,0:T(8,128)}, u32[]{:S(2)}, u32[]{:S(2)}) collective-permute-start(f32[8,64,256]{2,1,0:T(8,128)} %bitcast.3), channel_id=1, source_target_pairs={{0,3},{32,35},{64,67},{96,99}} | collective-permute-start | bytes 1572872 | tf_op jit(solution)/shard_map/ppermute | solution.py:314
  20.2 3.9 %all-to-all-start = ((f32[32,4,8,256]{3,2,1,0:T(8,128)}), f32[32,4,8,256]{3,2,1,0:T(8,128)S(1)}, u32[]{:S(2)}, u32[]{:S(2)}) async-start(f32[32,4,8,256]{3,2,1,0:T(8,128)} %broadcast_in_dim.11), calls=%async_computation | async-start | bytes 2097152 | tf_op jit(solution)/shard_map/all_to_all | solution.py:307
  26.8 5.4 %collective-permute-done.4 = f32[8,64,256]{2,1,0:T(8,128)} collective-permute-done((f32[8,64,256]{2,1,0:T(8,128)}, f32[8,64,256]{2,1,0:T(8,128)}, u32[]{:S(2)}, u32[]{:S(2)}) %collective-permute-start.4) | collective-permute-done | bytes 524320 | tf_op jit(solution)/shard_map/ppermute | solution.py:314
  38.3 4.9 %collective-permute-start.6 = (f32[64,256]{1,0:T(8,128)S(1)}, f32[64,256]{1,0:T(8,128)S(1)}, u32[]{:S(2)}, u32[]{:S(2)}) collective-permute-start(f32[64,256]{1,0:T(8,128)S(1)} %get-tuple-element.48), channel_id=1, source_target_pairs={{0,1},{3,9},{4,17},{1,25},{32,33},{35,41},{36,49},{33,57},{64,65},... | collective-permute-start | bytes 196616 | tf_op jit(solution)/shard_map/ppermute | solution.py:322
  48.6 10.7 %all_to_all.15 = f32[8,64,256]{2,1,0:T(8,128)S(1)} all-to-all(f32[8,64,256]{2,1,0:T(8,128)S(1)} %broadcast_in_dim.12), channel_id=1, replica_groups={{0,1,2,3,4,5,6,7},{8,9,10,11,12,13,14,15},{16,17,18,19,20,21,22,23},{24..., dimensions={0} | all-to-all | bytes 1048576 | tf_op jit(solution)/shard_map/all_to_all | solution.py:307
  60.8 3.6 %all-to-all-start.2 = ((f32[4,8,64,256]{3,2,1,0:T(8,128)}), f32[4,8,64,256]{3,2,1,0:T(8,128)S(1)}, u32[]{:S(2)}, u32[]{:S(2)}) async-start(f32[4,8,64,256]{3,2,1,0:T(8,128)} %broadcast_in_dim.14), calls=%async_computation.2 | async-start | bytes 4194304 | tf_op jit(solution)/shard_map/all_to_all | solution.py:307
  64.4 2.9 %collective-permute-start.1 = (f32[128,1536]{1,0:T(8,128)}, f32[128,1536]{1,0:T(8,128)}, u32[]{:S(2)}, u32[]{:S(2)}) collective-permute-start(f32[128,1536]{1,0:T(8,128)} %get-tuple-element.22.own_ref), channel_id=1, source_target_pairs={{0,16},{1,17},{2,18},{3,19},{4,20},{5,21},{6,22},{7,23},{8,24},{9,... | collective-permute-start | bytes 2359304 | tf_op jit(solution)/shard_map/ppermute | solution.py:289
  67.4 2.7 %dynamic-slice_bitcast_fusion = f32[1536,256]{1,0:T(8,128)} fusion(f32[4,3072,256]{2,1,0:T(8,128)} %panels_ref.5, s32[]{:T(128)S(6)} %select_n.38), kind=kLoop, calls=%fused_computation.1 | loop fusion | bytes 3145732 | tf_op jit(solution)/shard_map/squeeze | solution.py:365
  72.7 21.4 %symmetric_inverses.1.inverse_ref = f32[4,256,256]{2,1,0:T(8,128)S(1)} custom-call(f32[32,4,8,256]{3,2,1,0:T(8,128)S(1)} %copy-done.1), custom_call_target="tpu_custom_call" | custom-call | flops 1 | bytes 1 | tf_op jit(solution)/shard_map/symmetric_inverses/pallas_call | solution.py:112
  94.1 5.1 %collective-permute-done.1.received_ref = f32[128,1536]{1,0:T(8,128)} collective-permute-done((f32[128,1536]{1,0:T(8,128)}, f32[128,1536]{1,0:T(8,128)}, u32[]{:S(2)}, u32[]{:S(2)}) %collective-permute-start.1) | collective-permute-done | bytes 786464 | tf_op jit(solution)/shard_map/ppermute | solution.py:289
  99.2 2.8 %merge.9.own_ref = f32[128,1536]{1,0:T(8,128)} custom-call(f32[128,1536]{1,0:T(8,128)} %get-tuple-element.22.own_ref, f32[128,1536]{1,0:T(8,128)} %collective-permute-done.1.received_ref, s32[1,128]{1,0:T(1,128)S(1)} %get-tuple-element.59.map_ref), custom_call_target="tpu_custom_call" | custom-call | flops 1 | bytes 1 | tf_op jit(solution)/shard_map/merge/pallas_call | solution.py:149
  102.0 2.8 %merge.10.own_ref = f32[128,1536]{1,0:T(8,128)} custom-call(f32[128,1536]{1,0:T(8,128)} %merge.8.own_ref, f32[128,1536]{1,0:T(8,128)} %collective-permute-done.14.received_ref, s32[1,128]{1,0:T(1,128)S(1)} %get-tuple-element.58.map_ref), custom_call_target="tpu_custom_call" | custom-call | flops 1 | bytes 1 | tf_op jit(solution)/shard_map/merge/pallas_call | solution.py:149
  104.8 2.8 %collective-permute-start.19 = (f32[128,1536]{1,0:T(8,128)}, f32[128,1536]{1,0:T(8,128)}, u32[]{:S(2)}, u32[]{:S(2)}) collective-permute-start(f32[128,1536]{1,0:T(8,128)} %merge.10.own_ref), channel_id=1, source_target_pairs={{0,64},{32,96},{64,0},{96,32},{1,65},{33,97},{65,1},{97,33},{2,66}... | collective-permute-start | bytes 2359304 | tf_op jit(solution)/shard_map/ppermute | solution.py:289
  109.5 9.8 %lower_rows.2.rest_0_ = f32[512,3072]{1,0:T(8,128)} custom-call(f32[512,3072]{1,0:T(8,128)} %front_ref.3, f32[4,3072,256]{2,1,0:T(8,128)} %panels_ref.5, f32[4,512,256]{2,1,0:T(8,128)S(1)} %bitcast.60, f32[4,256,256]{2,1,0:T(8,128)S(1)} %symmetric_inverses.1.inverse_ref), custom_call_target="tpu_custom_call" | custom-call | flops 1 | bytes 1 | tf_op jit(solution)/shard_map/lower_rows/pallas_call | solution.py:198
  119.3 9.1 %collective-permute-done.13.received_ref = f32[128,1536]{1,0:T(8,128)} collective-permute-done((f32[128,1536]{1,0:T(8,128)}, f32[128,1536]{1,0:T(8,128)}, u32[]{:S(2)}, u32[]{:S(2)}) %collective-permute-start.13) | collective-permute-done | bytes 786464 | tf_op jit(solution)/shard_map/ppermute | solution.py:289
  132.2 9.8 %lower_rows.3.lower_ref = f32[512,3072]{1,0:T(8,128)} custom-call(f32[512,3072]{1,0:T(8,128)} %front_ref.3, f32[4,3072,256]{2,1,0:T(8,128)} %panels_ref.5, f32[4,512,256]{2,1,0:T(8,128)S(1)} %bitcast.61, f32[4,256,256]{2,1,0:T(8,128)S(1)} %symmetric_inverses.1.inverse_ref, f32[512,3072]{1,0:T(8,128)} %lower_rows.2.rest_0_), custom_call_target="tpu_custom_call", output_to_operand_aliasing={{}: (4, {})} | custom-call | flops 1 | bytes 1 | tf_op jit(solution)/shard_map/lower_rows/pallas_call | solution.py:198
  142.4 10.0 %collective-permute-start.20 = (f32[128,1024]{1,0:T(8,128)S(1)}, f32[128,1024]{1,0:T(8,128)S(1)}, u32[]{:S(2)}, u32[]{:S(2)}) collective-permute-start(f32[128,1024]{1,0:T(8,128)S(1)} %pad_maximum_fusion.own_ref), channel_id=1, source_target_pairs={{0,32},{32,0},{64,96},{96,64},{1,33},{33,1},{65,97},{97,65},{2,34}... | collective-permute-start | bytes 1572872 | tf_op jit(solution)/shard_map/ppermute | solution.py:289
  152.5 2.8 %collective-permute-start.15 = (f32[128,1536]{1,0:T(8,128)S(1)}, f32[128,1536]{1,0:T(8,128)S(1)}, u32[]{:S(2)}, u32[]{:S(2)}) collective-permute-start(f32[128,1536]{1,0:T(8,128)S(1)} %merge.11.own_ref), channel_id=1, source_target_pairs={{0,64},{32,96},{64,0},{96,32},{1,65},{33,97},{65,1},{97,33},{2,66}... | collective-permute-start | bytes 2359304 | tf_op jit(solution)/shard_map/ppermute | solution.py:289
  156.5 11.0 %upper_rows.1.rest_ref = f32[512,3072]{1,0:T(8,128)} custom-call(s32[1]{0:T(128)} %bitcast.19.core_ref, f32[4,3072,256]{2,1,0:T(8,128)} %panels_ref.5, f32[1536,256]{1,0:T(8,128)} %collective-permute-done.16.near_ref, f32[1536,256]{1,0:T(8,128)S(1)} %collective-permute-done.17.far_ref, ...), custom_call_target="tpu_custom_call", output_to_operand_aliasing={{}: (6, {})} | custom-call | flops 1 | bytes 1 | tf_op jit(solution)/shard_map/upper_rows/pallas_call | solution.py:241
  167.4 5.3 %collective-permute-done.15.received_ref = f32[128,1536]{1,0:T(8,128)S(1)} collective-permute-done((f32[128,1536]{1,0:T(8,128)S(1)}, f32[128,1536]{1,0:T(8,128)S(1)}, u32[]{:S(2)}, u32[]{:S(2)}) %collective-permute-start.15) | collective-permute-done | bytes 786464 | tf_op jit(solution)/shard_map/ppermute | solution.py:289
  174.6 2.6 %finished.2.rest_ref = f32[512,3072]{1,0:T(8,128)} custom-call(f32[128,1536]{1,0:T(8,128)S(1)} %merge.12.own_ref, f32[128,1536]{1,0:T(8,128)S(1)} %collective-permute-done.22.received_ref, s32[1,128]{1,0:T(1,128)S(1)} %get-tuple-element.56.map_ref, f32[512,3072]{1,0:T(8,128)} %upper_rows.1.rest_ref), custom_call_target="tpu_custom_call", output_to_operand_aliasing={{}: (3, {})} | custom-call | flops 1 | bytes 1 | tf_op jit(solution)/shard_map/finished/pallas_call | solution.py:275
  177.1 2.6 %finished.3 = f32[512,3072]{1,0:T(8,128)} custom-call(f32[128,1536]{1,0:T(8,128)S(1)} %merge.15.own_ref, f32[128,1536]{1,0:T(8,128)S(1)} %collective-permute-done.21.received_ref, s32[1,128]{1,0:T(1,128)S(1)} %get-tuple-element.56.map_ref, f32[512,3072]{1,0:T(8,128)} %finished.2.rest_ref), custom_call_target="tpu_custom_call", output_to_operand_aliasing={{}: (3, {})} | custom-call | flops 1 | bytes 1 | tf_op jit(solution)/shard_map/finished/pallas_call | solution.py:275
  (71 shorter events, 35.1 us)
Async XLA Ops:
  2.4 21.8 %collective-permute-start = (f32[128,1536]{1,0:T(8,128)S(1)}, f32[128,1536]{1,0:T(8,128)S(1)}, u32[]{:S(2)}, u32[]{:S(2)}) collective-permute-start(f32[128,1536]{1,0:T(8,128)S(1)} %get-tuple-element.43.own_ref), channel_id=1, source_target_pairs={{0,16},{1,17},{2,18},{3,19},{4,20},{5,21},{6,22},{7,23},{8,24},{9,... | collective-permute-start | bytes 2359304 | tf_op jit(solution)/shard_map/ppermute | solution.py:289
  9.5 16.1 %collective-permute-start.2 = (f32[8,64,256]{2,1,0:T(8,128)}, f32[8,64,256]{2,1,0:T(8,128)}, u32[]{:S(2)}, u32[]{:S(2)}) collective-permute-start(f32[8,64,256]{2,1,0:T(8,128)} %bitcast.3), channel_id=1, source_target_pairs={{0,3},{32,35},{64,67},{96,99}} | collective-permute-start | bytes 1572872 | tf_op jit(solution)/shard_map/ppermute | solution.py:314
  14.9 11.9 %collective-permute-start.3 = (f32[8,64,256]{2,1,0:T(8,128)}, f32[8,64,256]{2,1,0:T(8,128)}, u32[]{:S(2)}, u32[]{:S(2)}) collective-permute-start(f32[8,64,256]{2,1,0:T(8,128)} %bitcast.4), channel_id=1, source_target_pairs={{0,4},{32,36},{64,68},{96,100}} | collective-permute-start | bytes 1572872 | tf_op jit(solution)/shard_map/ppermute | solution.py:314
  17.0 15.2 %collective-permute-start.4 = (f32[8,64,256]{2,1,0:T(8,128)}, f32[8,64,256]{2,1,0:T(8,128)}, u32[]{:S(2)}, u32[]{:S(2)}) collective-permute-start(f32[8,64,256]{2,1,0:T(8,128)} %bitcast.5), channel_id=1, source_target_pairs={{0,1},{32,33},{64,65},{96,97}} | collective-permute-start | bytes 1572872 | tf_op jit(solution)/shard_map/ppermute | solution.py:314
  20.2 28.3 %all-to-all-start = ((f32[32,4,8,256]{3,2,1,0:T(8,128)}), f32[32,4,8,256]{3,2,1,0:T(8,128)S(1)}, u32[]{:S(2)}, u32[]{:S(2)}) async-start(f32[32,4,8,256]{3,2,1,0:T(8,128)} %broadcast_in_dim.11), calls=%async_computation | async-start | bytes 2097152 | tf_op jit(solution)/shard_map/all_to_all | solution.py:307
  33.8 9.5 %collective-permute-start.10 = (f32[64,256]{1,0:T(8,128)S(1)}, f32[64,256]{1,0:T(8,128)S(1)}, u32[]{:S(2)}, u32[]{:S(2)}) collective-permute-start(f32[64,256]{1,0:T(8,128)S(1)} %get-tuple-element.51), channel_id=1, source_target_pairs={{0,5},{3,13},{4,21},{1,29},{32,37},{35,45},{36,53},{33,61},{64,69}... | collective-permute-start | bytes 196616 | tf_op jit(solution)/shard_map/ppermute | solution.py:322
  35.1 9.5 %collective-permute-start.11 = (f32[64,256]{1,0:T(8,128)S(1)}, f32[64,256]{1,0:T(8,128)S(1)}, u32[]{:S(2)}, u32[]{:S(2)}) collective-permute-start(f32[64,256]{1,0:T(8,128)S(1)} %get-tuple-element.50), channel_id=1, source_target_pairs={{0,6},{3,14},{4,22},{1,30},{32,38},{35,46},{36,54},{33,62},{64,70}... | collective-permute-start | bytes 196616 | tf_op jit(solution)/shard_map/ppermute | solution.py:322
  36.4 9.5 %collective-permute-start.12 = (f32[64,256]{1,0:T(8,128)S(1)}, f32[64,256]{1,0:T(8,128)S(1)}, u32[]{:S(2)}, u32[]{:S(2)}) collective-permute-start(f32[64,256]{1,0:T(8,128)S(1)} %get-tuple-element.49), channel_id=1, source_target_pairs={{0,7},{3,15},{4,23},{1,31},{32,39},{35,47},{36,55},{33,63},{64,71}... | collective-permute-start | bytes 196616 | tf_op jit(solution)/shard_map/ppermute | solution.py:322
  37.7 9.5 %collective-permute-start.5 = (f32[64,256]{1,0:T(8,128)S(1)}, f32[64,256]{1,0:T(8,128)S(1)}, u32[]{:S(2)}, u32[]{:S(2)}) collective-permute-start(f32[64,256]{1,0:T(8,128)S(1)} %get-tuple-element.55), channel_id=1, source_target_pairs={{3,8},{4,16},{1,24},{35,40},{36,48},{33,56},{67,72},{68,80},{65,88... | collective-permute-start | bytes 196616 | tf_op jit(solution)/shard_map/ppermute | solution.py:322
  38.3 8.8 %collective-permute-start.6 = (f32[64,256]{1,0:T(8,128)S(1)}, f32[64,256]{1,0:T(8,128)S(1)}, u32[]{:S(2)}, u32[]{:S(2)}) collective-permute-start(f32[64,256]{1,0:T(8,128)S(1)} %get-tuple-element.48), channel_id=1, source_target_pairs={{0,1},{3,9},{4,17},{1,25},{32,33},{35,41},{36,49},{33,57},{64,65},... | collective-permute-start | bytes 196616 | tf_op jit(solution)/shard_map/ppermute | solution.py:322
  43.2 3.9 %collective-permute-start.7 = (f32[64,256]{1,0:T(8,128)S(1)}, f32[64,256]{1,0:T(8,128)S(1)}, u32[]{:S(2)}, u32[]{:S(2)}) collective-permute-start(f32[64,256]{1,0:T(8,128)S(1)} %get-tuple-element.54), channel_id=1, source_target_pairs={{0,2},{3,10},{4,18},{1,26},{32,34},{35,42},{36,50},{33,58},{64,66}... | collective-permute-start | bytes 196616 | tf_op jit(solution)/shard_map/ppermute | solution.py:322
  44.6 2.9 %collective-permute-start.8 = (f32[64,256]{1,0:T(8,128)S(1)}, f32[64,256]{1,0:T(8,128)S(1)}, u32[]{:S(2)}, u32[]{:S(2)}) collective-permute-start(f32[64,256]{1,0:T(8,128)S(1)} %get-tuple-element.53), channel_id=1, source_target_pairs={{0,3},{3,11},{4,19},{1,27},{32,35},{35,43},{36,51},{33,59},{64,67}... | collective-permute-start | bytes 196616 | tf_op jit(solution)/shard_map/ppermute | solution.py:322
  60.8 46.8 %all-to-all-start.2 = ((f32[4,8,64,256]{3,2,1,0:T(8,128)}), f32[4,8,64,256]{3,2,1,0:T(8,128)S(1)}, u32[]{:S(2)}, u32[]{:S(2)}) async-start(f32[4,8,64,256]{3,2,1,0:T(8,128)} %broadcast_in_dim.14), calls=%async_computation.2 | async-start | bytes 4194304 | tf_op jit(solution)/shard_map/all_to_all | solution.py:307
  64.4 34.8 %collective-permute-start.1 = (f32[128,1536]{1,0:T(8,128)}, f32[128,1536]{1,0:T(8,128)}, u32[]{:S(2)}, u32[]{:S(2)}) collective-permute-start(f32[128,1536]{1,0:T(8,128)} %get-tuple-element.22.own_ref), channel_id=1, source_target_pairs={{0,16},{1,17},{2,18},{3,19},{4,20},{5,21},{6,22},{7,23},{8,24},{9,... | collective-permute-start | bytes 2359304 | tf_op jit(solution)/shard_map/ppermute | solution.py:289
  67.4 34.6 %collective-permute-start.14 = (f32[128,1536]{1,0:T(8,128)}, f32[128,1536]{1,0:T(8,128)}, u32[]{:S(2)}, u32[]{:S(2)}) collective-permute-start(f32[128,1536]{1,0:T(8,128)} %merge.8.own_ref), channel_id=1, source_target_pairs={{0,1},{1,0},{2,3},{3,2},{4,5},{5,4},{6,7},{7,6},{8,9},{9,8},{10,11... | collective-permute-start | bytes 2359304 | tf_op jit(solution)/shard_map/ppermute | solution.py:289
  70.0 82.3 %collective-permute-start.16 = (f32[1536,256]{1,0:T(8,128)}, f32[1536,256]{1,0:T(8,128)}, u32[]{:S(2)}, u32[]{:S(2)}) collective-permute-start(f32[1536,256]{1,0:T(8,128)} %dynamic-slice_bitcast_fusion), channel_id=1, source_target_pairs={{0,1},{1,0},{2,3},{3,2},{4,5},{5,4},{6,7},{7,6},{8,9},{9,8},{10,11... | collective-permute-start | bytes 4718600 | tf_op jit(solution)/shard_map/ppermute | solution.py:289
  104.8 25.4 %collective-permute-start.19 = (f32[128,1536]{1,0:T(8,128)}, f32[128,1536]{1,0:T(8,128)}, u32[]{:S(2)}, u32[]{:S(2)}) collective-permute-start(f32[128,1536]{1,0:T(8,128)} %merge.10.own_ref), channel_id=1, source_target_pairs={{0,64},{32,96},{64,0},{96,32},{1,65},{33,97},{65,1},{97,33},{2,66}... | collective-permute-start | bytes 2359304 | tf_op jit(solution)/shard_map/ppermute | solution.py:289
  107.6 20.8 %collective-permute-start.13 = (f32[128,1536]{1,0:T(8,128)}, f32[128,1536]{1,0:T(8,128)}, u32[]{:S(2)}, u32[]{:S(2)}) collective-permute-start(f32[128,1536]{1,0:T(8,128)} %merge.9.own_ref), channel_id=1, source_target_pairs={{0,1},{1,0},{2,3},{3,2},{4,5},{5,4},{6,7},{7,6},{8,9},{9,8},{10,11... | collective-permute-start | bytes 2359304 | tf_op jit(solution)/shard_map/ppermute | solution.py:289
  109.1 32.9 %collective-permute-start.18 = (f32[128,768]{1,0:T(8,128)S(1)}, f32[128,768]{1,0:T(8,128)S(1)}, u32[]{:S(2)}, u32[]{:S(2)}) collective-permute-start(f32[128,768]{1,0:T(8,128)S(1)} %pad_maximum_fusion.1.own_ref), channel_id=1, source_target_pairs={{0,64},{32,96},{64,0},{96,32},{1,65},{33,97},{65,1},{97,33},{2,66}... | collective-permute-start | bytes 1179656 | tf_op jit(solution)/shard_map/ppermute | solution.py:289
  142.4 13.5 %collective-permute-start.20 = (f32[128,1024]{1,0:T(8,128)S(1)}, f32[128,1024]{1,0:T(8,128)S(1)}, u32[]{:S(2)}, u32[]{:S(2)}) collective-permute-start(f32[128,1024]{1,0:T(8,128)S(1)} %pad_maximum_fusion.own_ref), channel_id=1, source_target_pairs={{0,32},{32,0},{64,96},{96,64},{1,33},{33,1},{65,97},{97,65},{2,34}... | collective-permute-start | bytes 1572872 | tf_op jit(solution)/shard_map/ppermute | solution.py:289
  152.4 4.1 %collective-permute-start.17 = (f32[1536,256]{1,0:T(8,128)}, f32[1536,256]{1,0:T(8,128)S(1)}, u32[]{:S(2)}, u32[]{:S(2)}) collective-permute-start(f32[1536,256]{1,0:T(8,128)} %collective-permute-done.16.near_ref), channel_id=1, source_target_pairs={{0,32},{32,0},{64,96},{96,64},{1,33},{33,1},{65,97},{97,65},{2,34}... | collective-permute-start | bytes 4718600 | tf_op jit(solution)/shard_map/ppermute | solution.py:289
  152.5 20.2 %collective-permute-start.15 = (f32[128,1536]{1,0:T(8,128)S(1)}, f32[128,1536]{1,0:T(8,128)S(1)}, u32[]{:S(2)}, u32[]{:S(2)}) collective-permute-start(f32[128,1536]{1,0:T(8,128)S(1)} %merge.11.own_ref), channel_id=1, source_target_pairs={{0,64},{32,96},{64,0},{96,32},{1,65},{33,97},{65,1},{97,33},{2,66}... | collective-permute-start | bytes 2359304 | tf_op jit(solution)/shard_map/ppermute | solution.py:289
  155.2 19.3 %collective-permute-start.22 = (f32[128,1536]{1,0:T(8,128)S(1)}, f32[128,1536]{1,0:T(8,128)S(1)}, u32[]{:S(2)}, u32[]{:S(2)}) collective-permute-start(f32[128,1536]{1,0:T(8,128)S(1)} %merge.12.own_ref), channel_id=1, source_target_pairs={{0,32},{32,0},{64,96},{96,64},{1,33},{33,1},{65,97},{97,65},{2,34}... | collective-permute-start | bytes 2359304 | tf_op jit(solution)/shard_map/ppermute | solution.py:289
  173.2 3.9 %collective-permute-start.21 = (f32[128,1536]{1,0:T(8,128)S(1)}, f32[128,1536]{1,0:T(8,128)S(1)}, u32[]{:S(2)}, u32[]{:S(2)}) collective-permute-start(f32[128,1536]{1,0:T(8,128)S(1)} %merge.15.own_ref), channel_id=1, source_target_pairs={{0,32},{32,0},{64,96},{96,64},{1,33},{33,1},{65,97},{97,65},{2,34}... | collective-permute-start | bytes 2359304 | tf_op jit(solution)/shard_map/ppermute | solution.py:289
  (6 other events, 69.6 us)
